TPU v7x, 256 devices: a whole 4x4x8 slice. The times are simulated.
256 devices in a mesh: expert: 8 (over x, core), fsdp: 32 (over z, y).
Axes of the slice: x: 4, y: 4, z: 8, core: 2. Of those that a mesh axis runs over, the one named last changes fastest.
Arguments:
- teacher_tokens: bfloat16 [4096, 7168], P('fsdp'), may hold values from -6 to 6
- routes: int32 [4096, 8], P('fsdp'), may hold values from 0 to 255, as said below
- slots: int32 [4096, 8], P('fsdp'), may hold values from -1 to 3, as said below
- route_weights: float32 [4096, 8], P('fsdp'), may hold values from 0.1 to 1
- gate_proj: bfloat16 [32, 7168, 1024], P('fsdp', None, 'expert'), may hold values from -0.0625 to 0.0625
- up_proj: bfloat16 [32, 7168, 1024], P('fsdp', None, 'expert'), may hold values from -0.0625 to 0.0625
- down_proj: bfloat16 [32, 1024, 7168], P('fsdp', 'expert'), may hold values from -0.1875 to 0.1875
- projector: bfloat16 [7168, 5120], P('fsdp', 'expert'), may hold values from -0.0625 to 0.0625
- student_input: bfloat16 [4096, 5120], P('fsdp'), may hold values from -6 to 6
- student_weight: bfloat16 [5120, 5120], P('fsdp', 'expert'), may hold values from -0.078125 to 0.078125
Outputs:
- target: bfloat16 [4096, 5120], P('fsdp', 'expert')
- grad_weight: float32 [5120, 5120], P('fsdp', 'expert')
Inputs may be any that keep to these rules, and one draw needn't show every extreme that they name: `routes`: each row names 8 different experts. In each aligned block of 128 rows every expert below 32 is named by 1 to 4 rows, and some expert below 32, drawn from the seed, is named by exactly 4 rows in every block. `slots`: for a choice naming an expert below 32: its slot, different for the choices of one block that name that expert; -1 for every other choice.
All inputs are finite; a program needn't handle non-finite values.
Results may differ from a plain program's by a relative error of at most 0.02.
Values may be sent and summed in bfloat16 or wider, within the bound.
No kernel may reach another device: no remote copies, remote signals or barrier semaphores. Data moves between devices by JAX's collectives and lax.ppermute only.
A program may use at most 128 MiB of HBM per device.

v0:
```python
import math

import jax
import jax.numpy as jnp
from jax import lax
from jax.sharding import PartitionSpec as P

CAP = 4


def combine_rows(rows, slot_index, weights):
    running = jnp.zeros((slot_index.shape[0], rows.shape[1]), jnp.float32)
    for choice_index in range(slot_index.shape[1]):
        column = slot_index[:, choice_index]
        picked = jnp.take(rows, jnp.maximum(column, 0), axis=0).astype(jnp.float32)
        factor = jnp.where(column >= 0, weights[:, choice_index], 0.0)
        running = running + factor[:, None] * picked
    return running.astype(jnp.bfloat16)


def body(
    teacher_tokens,
    routes,
    slots,
    route_weights,
    gate_proj,
    up_proj,
    down_proj,
    projector,
    student_input,
    student_weight,
):
    owners = lax.axis_size("fsdp")
    tok_rows = teacher_tokens.shape[0]
    model_width = teacher_tokens.shape[1]
    slot_count = owners * CAP
    slot_ids = jnp.arange(slot_count, dtype=jnp.int32)
    slot_index = jnp.where(routes < owners, routes * CAP + slots, -1)
    matches = slot_index[:, :, None] == slot_ids
    dispatch_mask = jnp.sum(matches.astype(jnp.float32), axis=1).astype(jnp.bfloat16)
    outgoing = jnp.einsum(
        "tw,td->wd", dispatch_mask, teacher_tokens, preferred_element_type=jnp.float32
    ).astype(jnp.bfloat16)
    arrived = lax.all_to_all(
        outgoing.reshape(owners, CAP, model_width), "fsdp", split_axis=0, concat_axis=0, tiled=True
    ).reshape(slot_count, model_width)
    gate_act = jnp.dot(arrived, gate_proj[0], preferred_element_type=jnp.float32)
    up_act = jnp.dot(arrived, up_proj[0], preferred_element_type=jnp.float32)
    hidden = (jax.nn.silu(gate_act) * up_act).astype(jnp.bfloat16)
    partial_out = jnp.dot(hidden, down_proj[0], preferred_element_type=jnp.float32)
    summed = lax.psum(partial_out.astype(jnp.bfloat16), "expert")
    returned_rows = lax.all_to_all(
        summed.reshape(owners, CAP, model_width), "fsdp", split_axis=0, concat_axis=0, tiled=True
    ).reshape(slot_count, model_width)
    teacher_out = combine_rows(returned_rows, slot_index, route_weights)
    student_full, projector_full = (
        lax.all_gather(student_weight, "fsdp", axis=0, tiled=True),
        lax.all_gather(projector, "fsdp", axis=0, tiled=True),
    )
    projected = jnp.dot(teacher_out, projector_full, preferred_element_type=jnp.float32)
    student_out = jnp.dot(student_input, student_full, preferred_element_type=jnp.float32)
    error_scale = 1.0 / math.sqrt(tok_rows * owners)
    error = ((student_out - projected) * error_scale).astype(jnp.bfloat16)
    gradient = lax.psum_scatter(
        jnp.einsum("tc,td->cd", student_input, error, preferred_element_type=jnp.float32).astype(
            jnp.bfloat16
        ),
        "fsdp",
        scatter_dimension=0,
        tiled=True,
    ).astype(jnp.float32)
    return (projected.astype(jnp.bfloat16), gradient)


def solution(mesh):
    return jax.shard_map(
        body,
        mesh=mesh,
        in_specs=(
            P("fsdp", None),
            P("fsdp", None),
            P("fsdp", None),
            P("fsdp", None),
            P("fsdp", None, "expert"),
            P("fsdp", None, "expert"),
            P("fsdp", "expert", None),
            P("fsdp", "expert"),
            P("fsdp", None),
            P("fsdp", "expert"),
        ),
        out_specs=(P("fsdp", "expert"), P("fsdp", "expert")),
        check_vma=False,
    )
```

profile of v0, /device:TPU:96, one launch (start us, length us, event | category | flops | bytes accessed | tf_op | source)
XLA Modules:
  0.0 563.0 jit_solution(17756210367592120741)
XLA Ops:
  9.5 1.9 convolution_convert_fusion.1
  11.5 3.1 reshape.38
  14.6 54.2 %all_to_all.10 = bf16[32,4,7168]{2,1,0:T(4,128)(2,1)} all-to-all(bf16[32,4,7168]{2,1,0:T(4,128)(2,1)S(1)} %reshape.38), channel_id=1, replica_groups=mesh['expert'=8,'fsdp'=32] {'fsdp'}, dimensions={0} | all-to-all | bytes 3670016 | tf_op jit(solution)/shard_map/all_to_all | solution.py:44
  68.8 2.9 reshape.39
  71.8 2.1 fusion.4
  73.9 4.5 convolution_convert_fusion
  78.5 4.1 reshape.40
  83.8 68.2 %all-reduce.2.cloned.1.call-done = bf16[32,4,7168]{2,1,0:T(4,128)(2,1)} async-done(((bf16[32,4,7168]{2,1,0:T(4,128)(2,1)}), bf16[32,4,7168]{2,1,0:T(4,128)(2,1)}) %all-reduce.2.cloned.1.call-update) | async-done | bytes 1835024 | tf_op jit(solution)/shard_map/psum | solution.py:51
  152.0 9.7 %all-to-all-start.1 = ((bf16[32,4,7168]{2,1,0:T(4,128)(2,1)}), bf16[32,4,7168]{2,1,0:T(4,128)(2,1)}, u32[]{:S(2)}, u32[]{:S(2)}) async-start(bf16[32,4,7168]{2,1,0:T(4,128)(2,1)} %all-reduce.2.cloned.1.call-done), calls=%async_computation.1 | async-start | bytes 3670016 | tf_op jit(solution)/shard_map/all_to_all | solution.py:52
  162.0 61.3 %all-to-all-done.1 = bf16[32,4,7168]{2,1,0:T(4,128)(2,1)} async-done(((bf16[32,4,7168]{2,1,0:T(4,128)(2,1)}), bf16[32,4,7168]{2,1,0:T(4,128)(2,1)}, u32[]{:S(2)}, u32[]{:S(2)}) %all-to-all-start.1) | async-done | bytes 1835040 | tf_op jit(solution)/shard_map/all_to_all | solution.py:52
  223.3 2.9 reshape.41
  226.2 3.0 gather_fusion.2
  229.2 3.0 gather_fusion.3
  232.2 3.0 gather_fusion.4
  235.2 2.9 gather_fusion.5
  238.1 3.0 gather_fusion.6
  241.1 3.0 gather_fusion
  244.1 2.9 gather_fusion.1
  247.1 2.9 gather_fusion.7
  250.0 13.4 %fusion.37 = (bf16[128,640]{1,0:T(8,128)(2,1)}, f32[128,640]{1,0:T(8,128)S(1)}) fusion(bf16[7168,640]{1,0:T(8,128)(2,1)} %all-gather.3.cloned.1.call-done, bf16[128,7168]{1,0:T(8,128)(2,1)} %gather_fusion.7, bf16[128,7168]{1,0:T(8,128)(2,1)} %gather_fusion.6, bf16[128,7168]{1,0:T(8,128)(2,1)} %gather_fusion.5, bf16[128,7168]{1,0:T(8,128)(2,1)} %gather_fusion.4, ...), kind=kOutput, calls=%fused_computation.79 | convolution fusion | flops 1203847168 | bytes 24351744 | tf_op jit(solution)/shard_map/dot_general | solution.py:60
  263.4 50.0 %all-gather.5.cloned.1.call-done = bf16[5120,640]{1,0:T(8,128)(2,1)} async-done(((bf16[160,640]{1,0:T(8,128)(2,1)}), bf16[5120,640]{1,0:T(8,128)(2,1)}) %all-gather.5.cloned.1.call-update) | async-done | bytes 6553616 | tf_op jit(solution)/shard_map/all_gather | solution.py:57
  313.4 8.8 %fusion = bf16[5120,640]{0,1:T(8,128)(2,1)} fusion(bf16[128,5120]{1,0:T(8,128)(2,1)S(1)} %copy-done.2, f32[128,640]{1,0:T(8,128)S(1)} %get-tuple-element.48, bf16[5120,640]{1,0:T(8,128)(2,1)} %all-gather.5.cloned.1.call-done), kind=kOutput, calls=%fused_computation.11 | convolution fusion | flops 1681244160 | bytes 14745600 | tf_op jit(solution)/shard_map/tc,td->cd/dot_general | solution.py:65
  322.2 9.5 %copy.18 = bf16[5120,640]{1,0:T(8,128)(2,1)} copy(bf16[5120,640]{0,1:T(8,128)(2,1)} %fusion) | data formatting | bytes 13107200
  331.7 221.7 %reduce-scatter.4.cloned.1.call-done = bf16[160,640]{1,0:T(8,128)(2,1)} async-done(((bf16[5120,640]{1,0:T(8,128)(2,1)}), bf16[160,640]{1,0:T(8,128)(2,1)}) %reduce-scatter.4.cloned.1.call-update) | async-done | bytes 204816
  (28 shorter events, 5.0 us)
Async XLA Ops:
  8.0 1.5 copy-start
  8.0 144.0 %all-reduce.2.cloned.1.call-start = ((), (), s32[]{:S(2)}) async-start(), calls=%async_computation.3 | async-start | bytes 3670016 | tf_op jit(solution)/shard_map/psum | solution.py:51
  82.6 167.4 %all-gather.3.cloned.1.call-start = ((), (), s32[]{:S(2)}) async-start(), calls=%async_computation.4 | async-start | bytes 9461760 | tf_op jit(solution)/shard_map/all_gather | solution.py:58
  83.2 230.2 %all-gather.5.cloned.1.call-start = ((), (), s32[]{:S(2)}) async-start(), calls=%async_computation.5 | async-start | bytes 6758400 | tf_op jit(solution)/shard_map/all_gather | solution.py:57
  83.8 78.2 %copy-start.3 = (f32[128,8]{0,1:T(8,128)S(1)}, f32[128,8]{0,1:T(8,128)}, u32[]{:S(2)}) copy-start(f32[128,8]{0,1:T(8,128)} %param.15) | copy-start | bytes 12292
  152.0 71.3 %all-to-all-start.1 = ((bf16[32,4,7168]{2,1,0:T(4,128)(2,1)}), bf16[32,4,7168]{2,1,0:T(4,128)(2,1)}, u32[]{:S(2)}, u32[]{:S(2)}) async-start(bf16[32,4,7168]{2,1,0:T(4,128)(2,1)} %all-reduce.2.cloned.1.call-done), calls=%async_computation.1 | async-start | bytes 3670016 | tf_op jit(solution)/shard_map/all_to_all | solution.py:52
  161.7 391.7 %reduce-scatter.4.cloned.1.call-start = ((), (), s32[]{:S(2)}) async-start(), calls=%async_computation.6 | async-start | bytes 6758400
  250.0 63.4 %copy-start.2 = (bf16[128,5120]{1,0:T(8,128)(2,1)S(1)}, bf16[128,5120]{1,0:T(8,128)(2,1)}, u32[]{:S(2)}) copy-start(bf16[128,5120]{1,0:T(8,128)(2,1)} %param.20) | copy-start | bytes 3932164
  331.7 223.7 %copy-start.1 = (bf16[128,7168]{1,0:T(8,128)(2,1)S(1)}, bf16[128,7168]{1,0:T(8,128)(2,1)}, u32[]{:S(2)}) copy-start(bf16[128,7168]{1,0:T(8,128)(2,1)} %param.12) | copy-start | bytes 5505028
Sparse Core Ops, SparseCore 0:
  82.7 69.2 all-reduce.1
Sparse Core Ops, SparseCore 1:
  85.6 138.9 all-gather.2
  227.1 86.2 all-gather.4
  331.8 221.6 reduce-scatter.3
where the time goes:
time: 566 us; the launch traced here: 563 us
  waiting for transfers between devices  402 us (71%)
  blocking collectives  54.2 us (10%)
  local copies, waits for them, and re-layouts  48.8 us (9%)
  matrix products  30.8 us (5%)
  between operations  15.8 us (3%)
  starting transfers between devices  10 us (2%)
    unnamed x5, waiting for transfers between devices  223 us
    psum x1, waiting for transfers between devices, body(): summed = lax.psum(partial_out.astype(jnp.bfloat16), 'expert')  68.2 us
    all_to_all x1, waiting for transfers between devices, body(): lax.all_to_all(summed.reshape(owners, CAP, model_width), 'fsdp', split_ax...  61.3 us
    all_to_all x1, blocking collectives, body(): lax.all_to_all(outgoing.reshape(owners, CAP, model_width), 'fsdp', split_...  54.2 us
    all_gather x1, waiting for transfers between devices, body(): lax.all_gather(student_weight, 'fsdp', axis=0, tiled=True)  50 us
    gather x8, local copies, waits for them, and re-layouts, combine_rows(): picked = jnp.take(rows, jnp.maximum(column, 0), axis=0).astype(jnp.float32)  23.7 us
    dot_general x1, matrix products, body(): jnp.dot(teacher_out, projector_full, preferred_element_type=jnp.float32)  13.4 us
    unnamed x11, local copies, waits for them, and re-layouts  11.8 us
  transfers between devices with their start and end apart: 5, of which 4 were waited for; matrix products, arithmetic and copies ran while one was open for 7% of the time, Pallas kernels for 0%

commit v1 on v0

v1 whole, which is shorter than its diff:
```python
import math

import jax
import jax.numpy as jnp
from jax import lax
from jax.experimental import pallas as pl
from jax.experimental.pallas import tpu as pltpu
from jax.sharding import Mesh
from jax.sharding import PartitionSpec as P

CAP = 4
BF = jnp.bfloat16
F32 = jnp.float32
VMEM = pl.BlockSpec(memory_space=pltpu.VMEM)
SMEM = pl.BlockSpec(memory_space=pltpu.SMEM)
PARAMS = pltpu.CompilerParams(vmem_limit_bytes=48 * 1024 * 1024)


def shifted(value, axis, hop):
    size = lax.axis_size(axis)
    return lax.ppermute(value, axis, [(i, (i - hop) % size) for i in range(size)])


def gather_expert(value):
    own = [value] + [shifted(value, "x", hop) for hop in (1, 2, 3)]
    other = [shifted(block, "c", 1) for block in own]
    return own + other


def ffn_kernel(order, *refs):
    blocks, (gate, up, down, keep, send) = refs[:8], refs[8:]
    width = blocks[0].shape[1]
    gate_act = jnp.zeros((blocks[0].shape[0], gate.shape[1]), F32)
    up_act = jnp.zeros_like(gate_act)
    for k in range(8):
        rows = pl.ds(pl.multiple_of(order[k] * width, 128), width)
        block = blocks[k][...]
        gate_act += jnp.dot(block, gate[rows, :], preferred_element_type=F32)
        up_act += jnp.dot(block, up[rows, :], preferred_element_type=F32)
    hidden = (gate_act / (1.0 + jnp.exp(-gate_act)) * up_act).astype(BF)
    for k in (4, 5, 6, 7, 0, 1, 2, 3):
        cols = pl.ds(pl.multiple_of(order[k] * width, 128), width)
        part = jnp.dot(hidden, down[:, cols], preferred_element_type=F32).astype(BF)
        if k < 4:
            keep[k] = part
        else:
            send[k - 4] = part


def ffn(order, blocks, gate, up, down):
    rows, width = blocks[0].shape
    shape = jax.ShapeDtypeStruct((4, rows, width), BF)
    return pl.pallas_call(
        ffn_kernel,
        out_shape=(shape, shape),
        in_specs=[SMEM] + [VMEM] * 11,
        out_specs=(VMEM, VMEM),
        compiler_params=PARAMS,
        name="expert_ffn",
    )(order, *blocks, gate, up, down)


def fold_kernel(a, b, c, d, out):
    zs, ys, rows, width = out.shape
    total = (a[...].astype(F32) + b[...].astype(F32)) + (c[...].astype(F32) + d[...].astype(F32))
    for y in range(ys):
        part = total[:, y * width : (y + 1) * width]
        out[:, y] = part.reshape(zs, rows, width).astype(BF)


def fold(parts, zs, ys):
    rows, width = parts[0].shape
    return pl.pallas_call(
        fold_kernel,
        out_shape=jax.ShapeDtypeStruct((zs, ys, rows // zs, width // ys), BF),
        in_specs=[VMEM] * 4,
        out_specs=VMEM,
        compiler_params=PARAMS,
        name="sum_and_split",
    )(*parts)


def project_kernel(order, *refs):
    blocks, projector, outs = refs[:8], refs[8], refs[9:]
    total = jnp.zeros((blocks[0].shape[0], projector.shape[2]), F32)
    for k in range(8):
        total += jnp.dot(blocks[k][...], projector[order[k]], preferred_element_type=F32)
    rows = outs[0].shape[0]
    for i, out in enumerate(outs):
        out[...] = total[i * rows : (i + 1) * rows].astype(out.dtype)


def project(order, blocks, projector):
    tokens, cols = blocks[0].shape[0] // 4, projector.shape[2]
    return pl.pallas_call(
        project_kernel,
        out_shape=[jax.ShapeDtypeStruct((tokens, cols), F32)]
        + [jax.ShapeDtypeStruct((tokens, cols), BF)] * 3,
        in_specs=[SMEM] + [VMEM] * 9,
        out_specs=[VMEM] * 4,
        compiler_params=PARAMS,
        name="project",
    )(order, *blocks, projector)


def gradient_kernel(order, *refs):
    blocks, inputs_t, outs, errors, total = refs[:8], refs[8], refs[9:13], refs[13], refs[14]
    tokens = blocks[0].shape[0]
    for k in range(8):
        errors[pl.ds(pl.multiple_of(order[k] * tokens, 128), tokens), :] = blocks[k][...]
    total[...] = jnp.dot(inputs_t[...], errors[...], preferred_element_type=F32)
    rows = outs[0].shape[0]
    for i, out in enumerate(outs):
        out[...] = total[pl.ds(pl.multiple_of(order[8 + i] * rows, 32), rows), :].astype(out.dtype)


def gradient_parts(order, blocks, inputs_t):
    tokens, cols = blocks[0].shape
    rows = inputs_t.shape[0]
    return pl.pallas_call(
        gradient_kernel,
        out_shape=[jax.ShapeDtypeStruct((rows // 4, cols), F32)]
        + [jax.ShapeDtypeStruct((rows // 4, cols), BF)] * 3,
        in_specs=[SMEM] + [VMEM] * 9,
        out_specs=[VMEM] * 4,
        scratch_shapes=[pltpu.VMEM((8 * tokens, cols), BF), pltpu.VMEM((rows, cols), F32)],
        compiler_params=PARAMS,
        name="gradient",
    )(order, *blocks, inputs_t)


def body(
    teacher_tokens,
    routes,
    slots,
    route_weights,
    gate_proj,
    up_proj,
    down_proj,
    projector,
    student_input,
    student_weight,
):
    fsdp = ("z", "y")
    zs, ys = lax.axis_size("z"), lax.axis_size("y")
    x, c, z, y = (lax.axis_index(name) for name in ("x", "c", "z", "y"))
    owners = zs * ys
    tokens, model = teacher_tokens.shape
    width = model // 8
    slot_count = owners * CAP
    chips = (x + jnp.arange(4, dtype=jnp.int32)) % 4
    order = jnp.concatenate([chips * 2 + c, chips * 2 + (1 - c)])

    slot_index = jnp.where(routes < owners, routes * CAP + slots, -1).T
    slot_ids = jnp.arange(slot_count, dtype=jnp.int32)[:, None]
    mask = jnp.zeros((slot_count, tokens), F32)
    for k in range(slot_index.shape[0]):
        mask = mask + (slot_index[k][None, :] == slot_ids).astype(F32)
    my_cols = lax.dynamic_slice_in_dim(teacher_tokens, (x * 2 + c) * width, width, 1)
    outgoing = jnp.dot(mask.astype(BF), my_cols, preferred_element_type=F32).astype(BF)
    arrived = lax.all_to_all(
        outgoing.reshape(owners, CAP, width), fsdp, split_axis=0, concat_axis=0, tiled=True
    ).reshape(slot_count, width)

    projector_z = lax.all_gather(projector, "z", axis=0, tiled=True).reshape(
        zs, projector.shape[0], projector.shape[1]
    )
    weight_y = [student_weight] + [shifted(student_weight, "y", hop) for hop in (1, 2, 3)]
    weight_y = lax.dynamic_slice_in_dim(jnp.stack(weight_y * 2), (4 - y) % 4, 4, 0)
    weight_y = weight_y.reshape(ys * student_weight.shape[0], student_weight.shape[1])
    input_cols = student_input.shape[1] // zs
    inputs_z = lax.all_to_all(
        student_input.reshape(tokens, zs, input_cols).transpose(1, 0, 2),
        "z",
        split_axis=0,
        concat_axis=0,
        tiled=True,
    ).reshape(zs * tokens, input_cols)
    inputs_t = inputs_z.T
    student_part = jnp.dot(inputs_z, weight_y, preferred_element_type=F32).astype(BF)
    student_out = lax.psum_scatter(student_part, "z", scatter_dimension=0, tiled=True)

    row_index = jnp.where(routes < owners, routes * (ys * CAP) + slots, -1).T
    packed = jnp.concatenate([row_index.astype(F32), route_weights.T])
    combine_rows = []
    row_ids = jnp.arange(slot_count * ys, dtype=jnp.int32)[None, :]
    for hop in range(ys):
        plan = packed if hop == 0 else shifted(packed, "y", hop)
        base = ((y + hop) % ys) * CAP
        part = jnp.zeros((tokens, slot_count * ys), F32)
        for k in range(8):
            row = plan[k].astype(jnp.int32)
            row = jnp.where(row >= 0, row + base, -1)
            part = part + jnp.where(row[:, None] == row_ids, plan[8 + k][:, None], 0.0)
        combine_rows.append(part)
    combine = jnp.concatenate(combine_rows)
    combine_high = lax.reduce_precision(combine, 8, 7)
    combine_low = (combine - combine_high).astype(BF)
    combine_high = combine_high.astype(BF)

    blocks = gather_expert(arrived)
    keep, send = ffn(order, blocks, gate_proj[0], up_proj[0], down_proj[0])
    taken = shifted(send, "c", 1)
    pairs = [(keep[i].astype(F32) + taken[i].astype(F32)).astype(BF) for i in range(4)]
    parts = [pairs[0]] + [shifted(pairs[hop], "x", -hop) for hop in (1, 2, 3)]
    outgoing_rows = fold(parts, zs, ys)
    returned = lax.all_to_all(
        outgoing_rows.reshape(owners, ys * CAP, width // ys),
        fsdp,
        split_axis=0,
        concat_axis=0,
        tiled=True,
    ).reshape(slot_count * ys, width // ys)
    teacher = (
        jnp.dot(combine_high, returned, preferred_element_type=F32)
        + jnp.dot(combine_low, returned, preferred_element_type=F32)
    ).astype(BF)

    sums = project(order, gather_expert(teacher), projector_z)
    projected = sums[0]
    for hop in (1, 2, 3):
        projected = projected + shifted(sums[hop], "y", -hop).astype(F32)
    scale = 1.0 / math.sqrt(tokens * owners)
    error = ((student_out.astype(F32) - projected) * scale).astype(BF)

    ahead, behind = [error], [error]
    for hop in (1, 2, 3, 4):
        ahead.append(shifted(ahead[-1], "z", 1))
        if hop < 4:
            behind.append(shifted(behind[-1], "z", -1))
    errors = [error] + ahead[1:] + behind[1:]
    spots = jnp.array([0, 1, 2, 3, 4, -1, -2, -3], jnp.int32)
    grad_order = jnp.concatenate([(z + spots) % zs, (y + jnp.arange(4, dtype=jnp.int32)) % ys])
    grads = gradient_parts(grad_order, errors, inputs_t)
    gradient = grads[0]
    for hop in (1, 2, 3):
        gradient = gradient + shifted(grads[hop], "y", -hop).astype(F32)
    return (projected.astype(BF), gradient)


def solution(mesh):
    fine = Mesh(mesh.devices.reshape(4, 2, 8, 4), ("x", "c", "z", "y"))
    fsdp, expert = ("z", "y"), ("x", "c")
    return jax.shard_map(
        body,
        mesh=fine,
        in_specs=(
            P(fsdp, None),
            P(fsdp, None),
            P(fsdp, None),
            P(fsdp, None),
            P(fsdp, None, expert),
            P(fsdp, None, expert),
            P(fsdp, expert, None),
            P(fsdp, expert),
            P(fsdp, None),
            P(fsdp, expert),
        ),
        out_specs=(P(fsdp, expert), P(fsdp, expert)),
        check_vma=False,
    )
```

time: 566 us -> 213 us (0.38)
  waiting for transfers between devices: 402 us -> 80.3 us
  starting transfers between devices: 10 us -> 69.7 us
  blocking collectives: 54.2 us -> 0 us
  matrix products: 30.8 us -> 4.88 us
  local copies, waits for them, and re-layouts: 48.8 us -> 25.2 us
  Pallas kernels: 0 us -> 9.67 us
  other arithmetic: 1.13 us -> 8.08 us
    unnamed x5 -> x2, waiting for transfers between devices: 223 us -> 0.03 us
    psum x1 -> x0, waiting for transfers between devices: 68.2 us -> none  [body(): summed = lax.psum(partial_out.astype(jnp.bfloat16), 'expert')]
    all_to_all x1 -> x0, blocking collectives: 54.2 us -> none  [body(): lax.all_to_all(outgoing.reshape(owners, CAP, model_width), 'fsdp', split_...]
    ppermute x0 -> x37, waiting for transfers between devices: none -> 50.6 us  [shifted(): lax.ppermute(value, axis, [(i, (i - hop) % size) for i in range(size)])]
    all_gather x2 -> x1, waiting for transfers between devices: 50 us -> 0.01 us  [body(): lax.all_gather(projector, 'z', axis=0, tiled=True)]
    ppermute x0 -> x37, starting transfers between devices: none -> 44.5 us  [shifted(): lax.ppermute(value, axis, [(i, (i - hop) % size) for i in range(size)])]
    all_to_all x1 -> x3, waiting for transfers between devices: 61.3 us -> 29.7 us  [the longest x1 13.2 us: body(): lax.all_to_all(student_input.reshape(tokens, zs, input_cols).transpose(1,...]
    dot_general x5 -> x4, matrix products: 30.8 us -> 4.88 us  [the longest x1 4.04 us: body(): jnp.dot(inputs_z, weight_y, preferred_element_type=F32).astype(BF)]
  transfers between devices with their start and end apart: 5 -> 42, of which waited for: 4 -> 19; matrix products, arithmetic and copies ran while one was open for 7% -> 12% of each run, Pallas kernels for 0% -> 4%
where the time goes in v1:
time: 213 us; the launch traced here: 212 us
  waiting for transfers between devices  80.3 us (38%)
  starting transfers between devices  69.7 us (33%)
  local copies, waits for them, and re-layouts  25.2 us (12%)
  between operations  14.5 us (7%)
  Pallas kernels  9.67 us (5%)
  other arithmetic  8.08 us (4%)
  matrix products  4.88 us (2%)
    ppermute x37, waiting for transfers between devices, shifted(): lax.ppermute(value, axis, [(i, (i - hop) % size) for i in range(size)])  50.6 us
    ppermute x37, starting transfers between devices, shifted(): lax.ppermute(value, axis, [(i, (i - hop) % size) for i in range(size)])  44.5 us
    unnamed x50, local copies, waits for them, and re-layouts  19.4 us
    all_to_all x1, waiting for transfers between devices, body(): lax.all_to_all(student_input.reshape(tokens, zs, input_cols).transpose(1,...  13.2 us
    all_to_all x1, waiting for transfers between devices, body(): lax.all_to_all(outgoing_rows.reshape(owners, ys * CAP, width // ys), fsdp...  11.8 us
    all_to_all x1, starting transfers between devices, body(): lax.all_to_all(outgoing.reshape(owners, CAP, width), fsdp, split_axis=0,...  9.21 us
    all_to_all x1, starting transfers between devices, body(): lax.all_to_all(outgoing_rows.reshape(owners, ys * CAP, width // ys), fsdp...  9.03 us
    all_to_all x1, starting transfers between devices, body(): lax.all_to_all(student_input.reshape(tokens, zs, input_cols).transpose(1,...  6.95 us
  transfers between devices with their start and end apart: 42, of which 19 were waited for; matrix products, arithmetic and copies ran while one was open for 12% of the time, Pallas kernels for 4%

profile of v1, /device:TPU:96, one launch (start us, length us, event | category | flops | bytes accessed | tf_op | source)
XLA Modules:
  0.0 212.3 jit_solution(9580296089138937421)
XLA Ops:
  10.4 2.9 %collective-permute-start.1 = (f32[16,128]{1,0:T(8,128)S(1)}, f32[16,128]{1,0:T(8,128)S(1)}, u32[]{:S(2)}, u32[]{:S(2)}) collective-permute-start(f32[16,128]{1,0:T(8,128)S(1)} %pad_maximum_fusion.1), channel_id=1, source_target_pairs={{0,2},{1,3},{2,0},{3,1},{4,6},{5,7},{6,4},{7,5},{8,10},{9,11},{10,... | collective-permute-start | bytes 24584 | tf_op jit(solution)/shard_map/ppermute | solution.py:21
  18.5 9.2 %all-to-all-start = ((bf16[32,4,896]{2,1,0:T(4,128)(2,1)}), bf16[32,4,896]{2,1,0:T(4,128)(2,1)S(1)}, u32[]{:S(2)}, u32[]{:S(2)}) async-start(bf16[32,4,896]{2,1,0:T(4,128)(2,1)} %reshape.556), calls=%async_computation | async-start | bytes 458752 | tf_op jit(solution)/shard_map/all_to_all | solution.py:161
  33.5 4.8 %all-to-all-done = bf16[32,4,896]{2,1,0:T(4,128)(2,1)S(1)} async-done(((bf16[32,4,896]{2,1,0:T(4,128)(2,1)}), bf16[32,4,896]{2,1,0:T(4,128)(2,1)S(1)}, u32[]{:S(2)}, u32[]{:S(2)}) %all-to-all-start) | async-done | bytes 229408 | tf_op jit(solution)/shard_map/all_to_all | solution.py:161
  38.2 6.9 %all-to-all-start.2 = ((bf16[8,128,640]{1,2,0:T(8,128)(2,1)}), bf16[8,128,640]{1,2,0:T(8,128)(2,1)}, u32[]{:S(2)}, u32[]{:S(2)}) async-start(bf16[8,128,640]{1,2,0:T(8,128)(2,1)} %bitcast.91), calls=%async_computation.2 | async-start | bytes 2621440 | tf_op jit(solution)/shard_map/all_to_all | solution.py:172
  51.6 2.9 %collective-permute-start.3 = (bf16[128,896]{1,0:T(8,128)(2,1)S(1)}, bf16[128,896]{1,0:T(8,128)(2,1)S(1)}, u32[]{:S(2)}, u32[]{:S(2)}) collective-permute-start(bf16[128,896]{1,0:T(8,128)(2,1)S(1)} %reshape.557.refs_0_), channel_id=1, source_target_pairs={{0,192},{64,0},{128,64},{192,128},{1,193},{65,1},{129,65},{193,129... | collective-permute-start | bytes 688136 | tf_op jit(solution)/shard_map/ppermute | solution.py:21
  67.5 4.5 %expert_ffn.1 = (bf16[4,128,896]{2,1,0:T(8,128)(2,1)S(1)}, bf16[4,128,896]{2,1,0:T(8,128)(2,1)}) custom-call(s32[8]{0:T(128)S(1)} %pad_add_fusion.order, bf16[128,896]{1,0:T(8,128)(2,1)S(1)} %reshape.557.refs_0_, bf16[128,896]{1,0:T(8,128)(2,1)S(1)} %collective-permute-done.3.refs_1_, bf16[128,896]{1,0:T(8,128)(2,1)S(1)} %collective-permute-done.4.refs_2_, ...), custom_call_target="tpu_custom_call" | custom-call | tf_op jit(solution)/shard_map/expert_ffn/pallas_call | solution.py:53
  72.5 13.2 %all-to-all-done.2 = bf16[8,128,640]{1,2,0:T(8,128)(2,1)} async-done(((bf16[8,128,640]{1,2,0:T(8,128)(2,1)}), bf16[8,128,640]{1,2,0:T(8,128)(2,1)}, u32[]{:S(2)}, u32[]{:S(2)}) %all-to-all-start.2) | async-done | bytes 1310752 | tf_op jit(solution)/shard_map/all_to_all | solution.py:172
  85.7 4.0 %fusion = bf16[1024,640]{1,0:T(8,128)(2,1)} fusion(bf16[640,640]{1,0:T(8,128)(2,1)} %bitcast.200, bf16[8,128,640]{1,2,0:T(8,128)(2,1)} %all-to-all-done.2), kind=kOutput, calls=%fused_computation.3 | convolution fusion | flops 839516160 | bytes 3440640 | tf_op jit(solution)/shard_map/dot_general | solution.py:180
  94.0 2.7 %collective-permute-start.12 = (bf16[128,896]{1,0:T(8,128)(2,1)S(1)}, bf16[128,896]{1,0:T(8,128)(2,1)S(1)}, u32[]{:S(2)}, u32[]{:S(2)}) collective-permute-start(bf16[128,896]{1,0:T(8,128)(2,1)S(1)} %get-tuple-element.23), channel_id=1, source_target_pairs={{0,128},{64,192},{128,0},{192,64},{1,129},{65,193},{129,1},{193,65... | collective-permute-start | bytes 688136 | tf_op jit(solution)/shard_map/ppermute | solution.py:21
  104.0 9.0 %all-to-all-start.1 = ((bf16[32,16,224]{2,1,0:T(8,128)(2,1)}), bf16[32,16,224]{2,1,0:T(8,128)(2,1)S(1)}, u32[]{:S(2)}, u32[]{:S(2)}) async-start(bf16[32,16,224]{2,1,0:T(8,128)(2,1)} %bitcast.82), calls=%async_computation.1 | async-start | bytes 524288 | tf_op jit(solution)/shard_map/all_to_all | solution.py:207
  113.5 11.8 %all-to-all-done.1 = bf16[32,16,224]{2,1,0:T(8,128)(2,1)S(1)} async-done(((bf16[32,16,224]{2,1,0:T(8,128)(2,1)}), bf16[32,16,224]{2,1,0:T(8,128)(2,1)S(1)}, u32[]{:S(2)}, u32[]{:S(2)}) %all-to-all-start.1) | async-done | bytes 229408 | tf_op jit(solution)/shard_map/all_to_all | solution.py:207
  125.9 3.1 %collective-permute-start.14 = (bf16[512,224]{1,0:T(8,128)(2,1)S(1)}, bf16[512,224]{1,0:T(8,128)(2,1)S(1)}, u32[]{:S(2)}, u32[]{:S(2)}) collective-permute-start(bf16[512,224]{1,0:T(8,128)(2,1)S(1)} %fusion.2.refs_0_), channel_id=1, source_target_pairs={{0,192},{64,0},{128,64},{192,128},{1,193},{65,1},{129,65},{193,129... | collective-permute-start | bytes 688136 | tf_op jit(solution)/shard_map/ppermute | solution.py:21
  130.7 7.5 %collective-permute-done.14.refs_1_ = bf16[512,224]{1,0:T(8,128)(2,1)S(1)} collective-permute-done((bf16[512,224]{1,0:T(8,128)(2,1)S(1)}, bf16[512,224]{1,0:T(8,128)(2,1)S(1)}, u32[]{:S(2)}, u32[]{:S(2)}) %collective-permute-start.14) | collective-permute-done | bytes 229408 | tf_op jit(solution)/shard_map/ppermute | solution.py:21
  155.8 7.5 %collective-permute-done.21 = bf16[128,640]{1,0:T(8,128)(2,1)S(1)} collective-permute-done((bf16[128,640]{1,0:T(8,128)(2,1)S(1)}, bf16[128,640]{1,0:T(8,128)(2,1)S(1)}, u32[]{:S(2)}, u32[]{:S(2)}) %collective-permute-start.21) | collective-permute-done | bytes 163872 | tf_op jit(solution)/shard_map/ppermute | solution.py:21
  165.8 3.1 %collective-permute-start.31 = (bf16[128,640]{1,0:T(8,128)(2,1)S(1)}, bf16[128,640]{1,0:T(8,128)(2,1)S(1)}, u32[]{:S(2)}, u32[]{:S(2)}) collective-permute-start(bf16[128,640]{1,0:T(8,128)(2,1)S(1)} %get-tuple-element.26.refs_0_), channel_id=1, source_target_pairs={{0,4},{4,8},{8,12},{12,16},{16,20},{20,24},{24,28},{28,0},{1,5},{5... | collective-permute-start | bytes 491528 | tf_op jit(solution)/shard_map/ppermute | solution.py:21
  168.9 3.5 %collective-permute-done.27.refs_1_ = bf16[128,640]{1,0:T(8,128)(2,1)S(1)} collective-permute-done((bf16[128,640]{1,0:T(8,128)(2,1)S(1)}, bf16[128,640]{1,0:T(8,128)(2,1)S(1)}, u32[]{:S(2)}, u32[]{:S(2)}) %collective-permute-start.27) | collective-permute-done | bytes 163872 | tf_op jit(solution)/shard_map/ppermute | solution.py:21
  172.4 3.3 %collective-permute-start.32 = (bf16[128,640]{1,0:T(8,128)(2,1)S(1)}, bf16[128,640]{1,0:T(8,128)(2,1)S(1)}, u32[]{:S(2)}, u32[]{:S(2)}) collective-permute-start(bf16[128,640]{1,0:T(8,128)(2,1)S(1)} %collective-permute-done.31.refs_5_), channel_id=1, source_target_pairs={{0,4},{4,8},{8,12},{12,16},{16,20},{20,24},{24,28},{28,0},{1,5},{5... | collective-permute-start | bytes 491528 | tf_op jit(solution)/shard_map/ppermute | solution.py:21
  175.7 3.2 %collective-permute-done.28.refs_2_ = bf16[128,640]{1,0:T(8,128)(2,1)S(1)} collective-permute-done((bf16[128,640]{1,0:T(8,128)(2,1)S(1)}, bf16[128,640]{1,0:T(8,128)(2,1)S(1)}, u32[]{:S(2)}, u32[]{:S(2)}) %collective-permute-start.28) | collective-permute-done | bytes 163872 | tf_op jit(solution)/shard_map/ppermute | solution.py:21
  179.0 3.3 %collective-permute-start.33 = (bf16[128,640]{1,0:T(8,128)(2,1)S(1)}, bf16[128,640]{1,0:T(8,128)(2,1)S(1)}, u32[]{:S(2)}, u32[]{:S(2)}) collective-permute-start(bf16[128,640]{1,0:T(8,128)(2,1)S(1)} %collective-permute-done.32.refs_6_), channel_id=1, source_target_pairs={{0,4},{4,8},{8,12},{12,16},{16,20},{20,24},{24,28},{28,0},{1,5},{5... | collective-permute-start | bytes 491528 | tf_op jit(solution)/shard_map/ppermute | solution.py:21
  182.2 3.2 %collective-permute-done.29.refs_3_ = bf16[128,640]{1,0:T(8,128)(2,1)S(1)} collective-permute-done((bf16[128,640]{1,0:T(8,128)(2,1)S(1)}, bf16[128,640]{1,0:T(8,128)(2,1)S(1)}, u32[]{:S(2)}, u32[]{:S(2)}) %collective-permute-start.29) | collective-permute-done | bytes 163872 | tf_op jit(solution)/shard_map/ppermute | solution.py:21
  187.0 5.0 %collective-permute-done.30.refs_4_ = bf16[128,640]{1,0:T(8,128)(2,1)S(1)} collective-permute-done((bf16[128,640]{1,0:T(8,128)(2,1)S(1)}, bf16[128,640]{1,0:T(8,128)(2,1)S(1)}, u32[]{:S(2)}, u32[]{:S(2)}) %collective-permute-start.30) | collective-permute-done | bytes 163872 | tf_op jit(solution)/shard_map/ppermute | solution.py:21
  195.1 3.6 %collective-permute-start.35 = (bf16[160,640]{1,0:T(8,128)(2,1)S(1)}, bf16[160,640]{1,0:T(8,128)(2,1)S(1)}, u32[]{:S(2)}, u32[]{:S(2)}) collective-permute-start(bf16[160,640]{1,0:T(8,128)(2,1)S(1)} %get-tuple-element.20), channel_id=1, source_target_pairs={{0,2},{1,3},{2,0},{3,1},{4,6},{5,7},{6,4},{7,5},{8,10},{9,11},{10,... | collective-permute-start | bytes 614408 | tf_op jit(solution)/shard_map/ppermute | solution.py:21
  198.7 2.9 %collective-permute-done.34 = bf16[160,640]{1,0:T(8,128)(2,1)S(1)} collective-permute-done((bf16[160,640]{1,0:T(8,128)(2,1)S(1)}, bf16[160,640]{1,0:T(8,128)(2,1)S(1)}, u32[]{:S(2)}, u32[]{:S(2)}) %collective-permute-start.34) | collective-permute-done | bytes 204832 | tf_op jit(solution)/shard_map/ppermute | solution.py:21
  201.5 3.1 %collective-permute-done.35 = bf16[160,640]{1,0:T(8,128)(2,1)S(1)} collective-permute-done((bf16[160,640]{1,0:T(8,128)(2,1)S(1)}, bf16[160,640]{1,0:T(8,128)(2,1)S(1)}, u32[]{:S(2)}, u32[]{:S(2)}) %collective-permute-start.35) | collective-permute-done | bytes 204832 | tf_op jit(solution)/shard_map/ppermute | solution.py:21
  (147 shorter events, 73.7 us)
Async XLA Ops:
  7.2 136.9 %all-gather.2.cloned.1.call-start = ((), (), s32[]{:S(2)}) async-start(), calls=%async_computation.4 | async-start | bytes 2580480 | tf_op jit(solution)/shard_map/all_gather | solution.py:165
  8.9 23.1 %collective-permute-start.2 = (f32[16,128]{1,0:T(8,128)S(1)}, f32[16,128]{1,0:T(8,128)S(1)}, u32[]{:S(2)}, u32[]{:S(2)}) collective-permute-start(f32[16,128]{1,0:T(8,128)S(1)} %pad_maximum_fusion.1), channel_id=1, source_target_pairs={{0,1},{1,2},{2,3},{3,0},{4,5},{5,6},{6,7},{7,4},{8,9},{9,10},{10,1... | collective-permute-start | bytes 24584 | tf_op jit(solution)/shard_map/ppermute | solution.py:21
  10.4 34.8 %collective-permute-start.1 = (f32[16,128]{1,0:T(8,128)S(1)}, f32[16,128]{1,0:T(8,128)S(1)}, u32[]{:S(2)}, u32[]{:S(2)}) collective-permute-start(f32[16,128]{1,0:T(8,128)S(1)} %pad_maximum_fusion.1), channel_id=1, source_target_pairs={{0,2},{1,3},{2,0},{3,1},{4,6},{5,7},{6,4},{7,5},{8,10},{9,11},{10,... | collective-permute-start | bytes 24584 | tf_op jit(solution)/shard_map/ppermute | solution.py:21
  13.3 76.4 %collective-permute-start = (f32[16,128]{1,0:T(8,128)S(1)}, f32[16,128]{1,0:T(8,128)S(1)}, u32[]{:S(2)}, u32[]{:S(2)}) collective-permute-start(f32[16,128]{1,0:T(8,128)S(1)} %pad_maximum_fusion.1), channel_id=1, source_target_pairs={{0,3},{1,0},{2,1},{3,2},{4,7},{5,4},{6,5},{7,6},{8,11},{9,8},{10,9... | collective-permute-start | bytes 24584 | tf_op jit(solution)/shard_map/ppermute | solution.py:21
  14.7 30.6 %collective-permute-start.24 = (bf16[160,640]{1,0:T(8,128)(2,1)}, bf16[160,640]{1,0:T(8,128)(2,1)}, u32[]{:S(2)}, u32[]{:S(2)}) collective-permute-start(bf16[160,640]{1,0:T(8,128)(2,1)} %param.20), channel_id=1, source_target_pairs={{0,3},{1,0},{2,1},{3,2},{4,7},{5,4},{6,5},{7,6},{8,11},{9,8},{10,9... | collective-permute-start | bytes 614408 | tf_op jit(solution)/shard_map/ppermute | solution.py:21
  14.7 32.2 %collective-permute-start.25 = (bf16[160,640]{1,0:T(8,128)(2,1)}, bf16[160,640]{1,0:T(8,128)(2,1)}, u32[]{:S(2)}, u32[]{:S(2)}) collective-permute-start(bf16[160,640]{1,0:T(8,128)(2,1)} %param.20), channel_id=1, source_target_pairs={{0,2},{1,3},{2,0},{3,1},{4,6},{5,7},{6,4},{7,5},{8,10},{9,11},{10,... | collective-permute-start | bytes 614408 | tf_op jit(solution)/shard_map/ppermute | solution.py:21
  18.5 19.7 %all-to-all-start = ((bf16[32,4,896]{2,1,0:T(4,128)(2,1)}), bf16[32,4,896]{2,1,0:T(4,128)(2,1)S(1)}, u32[]{:S(2)}, u32[]{:S(2)}) async-start(bf16[32,4,896]{2,1,0:T(4,128)(2,1)} %reshape.556), calls=%async_computation | async-start | bytes 458752 | tf_op jit(solution)/shard_map/all_to_all | solution.py:161
  32.0 16.5 %collective-permute-start.26 = (bf16[160,640]{1,0:T(8,128)(2,1)}, bf16[160,640]{1,0:T(8,128)(2,1)S(1)}, u32[]{:S(2)}, u32[]{:S(2)}) collective-permute-start(bf16[160,640]{1,0:T(8,128)(2,1)} %param.20), channel_id=1, source_target_pairs={{0,1},{1,2},{2,3},{3,0},{4,5},{5,6},{6,7},{7,4},{8,9},{9,10},{10,1... | collective-permute-start | bytes 614408 | tf_op jit(solution)/shard_map/ppermute | solution.py:21
  38.2 47.4 %all-to-all-start.2 = ((bf16[8,128,640]{1,2,0:T(8,128)(2,1)}), bf16[8,128,640]{1,2,0:T(8,128)(2,1)}, u32[]{:S(2)}, u32[]{:S(2)}) async-start(bf16[8,128,640]{1,2,0:T(8,128)(2,1)} %bitcast.91), calls=%async_computation.2 | async-start | bytes 2621440 | tf_op jit(solution)/shard_map/all_to_all | solution.py:172
  45.2 118.8 %reduce-scatter.2.cloned.1.call-start = ((), (), s32[]{:S(2)}) async-start(), calls=%async_computation.5 | async-start | bytes 1474560 | tf_op jit(solution)/shard_map/reduce_scatter | solution.py:181
  51.6 9.0 %collective-permute-start.3 = (bf16[128,896]{1,0:T(8,128)(2,1)S(1)}, bf16[128,896]{1,0:T(8,128)(2,1)S(1)}, u32[]{:S(2)}, u32[]{:S(2)}) collective-permute-start(bf16[128,896]{1,0:T(8,128)(2,1)S(1)} %reshape.557.refs_0_), channel_id=1, source_target_pairs={{0,192},{64,0},{128,64},{192,128},{1,193},{65,1},{129,65},{193,129... | collective-permute-start | bytes 688136 | tf_op jit(solution)/shard_map/ppermute | solution.py:21
  55.4 9.1 %collective-permute-start.5 = (bf16[128,896]{1,0:T(8,128)(2,1)S(1)}, bf16[128,896]{1,0:T(8,128)(2,1)S(1)}, u32[]{:S(2)}, u32[]{:S(2)}) collective-permute-start(bf16[128,896]{1,0:T(8,128)(2,1)S(1)} %reshape.557.refs_0_), channel_id=1, source_target_pairs={{0,64},{64,128},{128,192},{192,0},{1,65},{65,129},{129,193},{193,1... | collective-permute-start | bytes 688136 | tf_op jit(solution)/shard_map/ppermute | solution.py:21
  57.9 9.5 %collective-permute-start.6 = (bf16[128,896]{1,0:T(8,128)(2,1)S(1)}, bf16[128,896]{1,0:T(8,128)(2,1)S(1)}, u32[]{:S(2)}, u32[]{:S(2)}) collective-permute-start(bf16[128,896]{1,0:T(8,128)(2,1)S(1)} %reshape.557.refs_0_), channel_id=1, source_target_pairs={{0,32},{32,0},{1,33},{33,1},{2,34},{34,2},{3,35},{35,3},{4,36},{36... | collective-permute-start | bytes 688136 | tf_op jit(solution)/shard_map/ppermute | solution.py:21
  72.0 18.8 %collective-permute-start.10 = (bf16[4,128,896]{2,1,0:T(8,128)(2,1)}, bf16[4,128,896]{2,1,0:T(8,128)(2,1)}, u32[]{:S(2)}, u32[]{:S(2)}) collective-permute-start(bf16[4,128,896]{2,1,0:T(8,128)(2,1)} %get-tuple-element.13), channel_id=1, source_target_pairs={{0,32},{32,0},{1,33},{33,1},{2,34},{34,2},{3,35},{35,3},{4,36},{36... | collective-permute-start | bytes 2752520 | tf_op jit(solution)/shard_map/ppermute | solution.py:21
  94.0 9.2 %collective-permute-start.12 = (bf16[128,896]{1,0:T(8,128)(2,1)S(1)}, bf16[128,896]{1,0:T(8,128)(2,1)S(1)}, u32[]{:S(2)}, u32[]{:S(2)}) collective-permute-start(bf16[128,896]{1,0:T(8,128)(2,1)S(1)} %get-tuple-element.23), channel_id=1, source_target_pairs={{0,128},{64,192},{128,0},{192,64},{1,129},{65,193},{129,1},{193,65... | collective-permute-start | bytes 688136 | tf_op jit(solution)/shard_map/ppermute | solution.py:21
  104.0 21.2 %all-to-all-start.1 = ((bf16[32,16,224]{2,1,0:T(8,128)(2,1)}), bf16[32,16,224]{2,1,0:T(8,128)(2,1)S(1)}, u32[]{:S(2)}, u32[]{:S(2)}) async-start(bf16[32,16,224]{2,1,0:T(8,128)(2,1)} %bitcast.82), calls=%async_computation.1 | async-start | bytes 524288 | tf_op jit(solution)/shard_map/all_to_all | solution.py:207
  125.9 12.3 %collective-permute-start.14 = (bf16[512,224]{1,0:T(8,128)(2,1)S(1)}, bf16[512,224]{1,0:T(8,128)(2,1)S(1)}, u32[]{:S(2)}, u32[]{:S(2)}) collective-permute-start(bf16[512,224]{1,0:T(8,128)(2,1)S(1)} %fusion.2.refs_0_), channel_id=1, source_target_pairs={{0,192},{64,0},{128,64},{192,128},{1,193},{65,1},{129,65},{193,129... | collective-permute-start | bytes 688136 | tf_op jit(solution)/shard_map/ppermute | solution.py:21
  129.0 9.6 %collective-permute-start.15 = (bf16[512,224]{1,0:T(8,128)(2,1)S(1)}, bf16[512,224]{1,0:T(8,128)(2,1)S(1)}, u32[]{:S(2)}, u32[]{:S(2)}) collective-permute-start(bf16[512,224]{1,0:T(8,128)(2,1)S(1)} %fusion.2.refs_0_), channel_id=1, source_target_pairs={{0,128},{64,192},{128,0},{192,64},{1,129},{65,193},{129,1},{193,65... | collective-permute-start | bytes 688136 | tf_op jit(solution)/shard_map/ppermute | solution.py:21
  130.7 10.5 %collective-permute-start.16 = (bf16[512,224]{1,0:T(8,128)(2,1)S(1)}, bf16[512,224]{1,0:T(8,128)(2,1)S(1)}, u32[]{:S(2)}, u32[]{:S(2)}) collective-permute-start(bf16[512,224]{1,0:T(8,128)(2,1)S(1)} %fusion.2.refs_0_), channel_id=1, source_target_pairs={{0,64},{64,128},{128,192},{192,0},{1,65},{65,129},{129,193},{193,1... | collective-permute-start | bytes 688136 | tf_op jit(solution)/shard_map/ppermute | solution.py:21
  130.7 10.5 %collective-permute-start.17 = (bf16[512,224]{1,0:T(8,128)(2,1)S(1)}, bf16[512,224]{1,0:T(8,128)(2,1)S(1)}, u32[]{:S(2)}, u32[]{:S(2)}) collective-permute-start(bf16[512,224]{1,0:T(8,128)(2,1)S(1)} %fusion.2.refs_0_), channel_id=1, source_target_pairs={{0,32},{32,0},{1,33},{33,1},{2,34},{34,2},{3,35},{35,3},{4,36},{36... | collective-permute-start | bytes 688136 | tf_op jit(solution)/shard_map/ppermute | solution.py:21
  151.9 11.4 %collective-permute-start.21 = (bf16[128,640]{1,0:T(8,128)(2,1)S(1)}, bf16[128,640]{1,0:T(8,128)(2,1)S(1)}, u32[]{:S(2)}, u32[]{:S(2)}) collective-permute-start(bf16[128,640]{1,0:T(8,128)(2,1)S(1)} %get-tuple-element.15), channel_id=1, source_target_pairs={{0,1},{1,2},{2,3},{3,0},{4,5},{5,6},{6,7},{7,4},{8,9},{9,10},{10,1... | collective-permute-start | bytes 491528 | tf_op jit(solution)/shard_map/ppermute | solution.py:21
  152.0 11.3 %collective-permute-start.22 = (bf16[128,640]{1,0:T(8,128)(2,1)S(1)}, bf16[128,640]{1,0:T(8,128)(2,1)S(1)}, u32[]{:S(2)}, u32[]{:S(2)}) collective-permute-start(bf16[128,640]{1,0:T(8,128)(2,1)S(1)} %get-tuple-element.16), channel_id=1, source_target_pairs={{0,2},{1,3},{2,0},{3,1},{4,6},{5,7},{6,4},{7,5},{8,10},{9,11},{10,... | collective-permute-start | bytes 491528 | tf_op jit(solution)/shard_map/ppermute | solution.py:21
  154.5 9.5 %collective-permute-start.23 = (bf16[128,640]{1,0:T(8,128)(2,1)S(1)}, bf16[128,640]{1,0:T(8,128)(2,1)S(1)}, u32[]{:S(2)}, u32[]{:S(2)}) collective-permute-start(bf16[128,640]{1,0:T(8,128)(2,1)S(1)} %get-tuple-element.17), channel_id=1, source_target_pairs={{0,3},{1,0},{2,1},{3,2},{4,7},{5,4},{6,5},{7,6},{8,11},{9,8},{10,9... | collective-permute-start | bytes 491528 | tf_op jit(solution)/shard_map/ppermute | solution.py:21
  195.1 9.5 %collective-permute-start.35 = (bf16[160,640]{1,0:T(8,128)(2,1)S(1)}, bf16[160,640]{1,0:T(8,128)(2,1)S(1)}, u32[]{:S(2)}, u32[]{:S(2)}) collective-permute-start(bf16[160,640]{1,0:T(8,128)(2,1)S(1)} %get-tuple-element.20), channel_id=1, source_target_pairs={{0,2},{1,3},{2,0},{3,1},{4,6},{5,7},{6,4},{7,5},{8,10},{9,11},{10,... | collective-permute-start | bytes 614408 | tf_op jit(solution)/shard_map/ppermute | solution.py:21
  (39 other events, 357.3 us)
Sparse Core Ops, SparseCore 0:
  17.6 65.0 all-gather.1
  89.9 39.8 reduce-scatter.1

commit v2 on v1

--- a/solution.py
+++ b/solution.py
@@ -13,7 +13,18 @@
 F32 = jnp.float32
 VMEM = pl.BlockSpec(memory_space=pltpu.VMEM)
 SMEM = pl.BlockSpec(memory_space=pltpu.SMEM)
-PARAMS = pltpu.CompilerParams(vmem_limit_bytes=48 * 1024 * 1024)
+
+
+def limit(mib):
+    return pltpu.CompilerParams(vmem_limit_bytes=mib * 1024 * 1024)
+
+
+def after(value, *earlier):
+    return lax.optimization_barrier((value, *earlier))[0]
+
+
+def in_hbm(value):
+    return pltpu.with_memory_space_constraint(value, pltpu.HBM)
 
 
 def shifted(value, axis, hop):
@@ -28,15 +39,28 @@
 
 
 def ffn_kernel(order, *refs):
-    blocks, (gate, up, down, keep, send) = refs[:8], refs[8:]
+    blocks, hbm, (keep, send), (gate, up, down, sems) = refs[:8], refs[8:11], refs[11:13], refs[13:]
     width = blocks[0].shape[1]
+
+    def rows(k):
+        return pl.ds(pl.multiple_of(order[k] * width, 128), width)
+
+    copies = [
+        pltpu.make_async_copy(hbm[i].at[rows(k), :], target.at[rows(k), :], sems.at[2 * k + i])
+        for k in range(8)
+        for i, target in enumerate((gate, up))
+    ] + [pltpu.make_async_copy(hbm[2], down, sems.at[16])]
+    for copy in copies:
+        copy.start()
     gate_act = jnp.zeros((blocks[0].shape[0], gate.shape[1]), F32)
     up_act = jnp.zeros_like(gate_act)
     for k in range(8):
-        rows = pl.ds(pl.multiple_of(order[k] * width, 128), width)
+        copies[2 * k].wait()
+        copies[2 * k + 1].wait()
         block = blocks[k][...]
-        gate_act += jnp.dot(block, gate[rows, :], preferred_element_type=F32)
-        up_act += jnp.dot(block, up[rows, :], preferred_element_type=F32)
+        gate_act += jnp.dot(block, gate[rows(k), :], preferred_element_type=F32)
+        up_act += jnp.dot(block, up[rows(k), :], preferred_element_type=F32)
+    copies[16].wait()
     hidden = (gate_act / (1.0 + jnp.exp(-gate_act)) * up_act).astype(BF)
     for k in (4, 5, 6, 7, 0, 1, 2, 3):
         cols = pl.ds(pl.multiple_of(order[k] * width, 128), width)
@@ -53,11 +77,13 @@
     return pl.pallas_call(
         ffn_kernel,
         out_shape=(shape, shape),
-        in_specs=[SMEM] + [VMEM] * 11,
+        in_specs=[SMEM] + [VMEM] * 8 + [pl.BlockSpec(memory_space=pltpu.HBM)] * 3,
         out_specs=(VMEM, VMEM),
-        compiler_params=PARAMS,
+        scratch_shapes=[pltpu.VMEM(weight.shape, BF) for weight in (gate, up, down)]
+        + [pltpu.SemaphoreType.DMA((17,))],
+        compiler_params=limit(16),
         name="expert_ffn",
-    )(order, *blocks, gate, up, down)
+    )(order, *blocks, in_hbm(gate), in_hbm(up), in_hbm(down))
 
 
 def fold_kernel(a, b, c, d, out):
@@ -75,7 +101,7 @@
         out_shape=jax.ShapeDtypeStruct((zs, ys, rows // zs, width // ys), BF),
         in_specs=[VMEM] * 4,
         out_specs=VMEM,
-        compiler_params=PARAMS,
+        compiler_params=limit(8),
         name="sum_and_split",
     )(*parts)
 
@@ -98,7 +124,7 @@
         + [jax.ShapeDtypeStruct((tokens, cols), BF)] * 3,
         in_specs=[SMEM] + [VMEM] * 9,
         out_specs=[VMEM] * 4,
-        compiler_params=PARAMS,
+        compiler_params=limit(12),
         name="project",
     )(order, *blocks, projector)
 
@@ -124,9 +150,38 @@
         in_specs=[SMEM] + [VMEM] * 9,
         out_specs=[VMEM] * 4,
         scratch_shapes=[pltpu.VMEM((8 * tokens, cols), BF), pltpu.VMEM((rows, cols), F32)],
-        compiler_params=PARAMS,
+        compiler_params=limit(16),
         name="gradient",
     )(order, *blocks, inputs_t)
+
+
+def student_kernel(order, *refs):
+    halves, gathered, part, inputs, weight = refs[:2], refs[2], refs[3], refs[4], refs[5]
+    tokens = halves[0].shape[1]
+    for k in range(2):
+        inputs[:, pl.ds(pl.multiple_of(order[k] * tokens, 32), tokens), :] = halves[k][...]
+    rows = weight.shape[0] // 4
+    for k in range(4):
+        weight[k * rows : (k + 1) * rows, :] = gathered[k, :rows, :]
+    flat = inputs[...].reshape(part.shape[0], weight.shape[0])
+    part[...] = jnp.dot(flat, weight[...], preferred_element_type=F32).astype(BF)
+
+
+def student(order, halves, gathered):
+    zs, tokens, width = halves[0].shape
+    cols = gathered.shape[2]
+    return pl.pallas_call(
+        student_kernel,
+        out_shape=(
+            jax.ShapeDtypeStruct((zs * 2 * tokens, cols), BF),
+            jax.ShapeDtypeStruct((zs, 2 * tokens, width), BF),
+        ),
+        in_specs=[SMEM] + [VMEM] * 3,
+        out_specs=(VMEM, VMEM),
+        scratch_shapes=[pltpu.VMEM((width, cols), BF)],
+        compiler_params=limit(16),
+        name="student",
+    )(order, *halves, gathered)
 
 
 def body(
@@ -151,6 +206,16 @@
     chips = (x + jnp.arange(4, dtype=jnp.int32)) % 4
     order = jnp.concatenate([chips * 2 + c, chips * 2 + (1 - c)])
 
+    weight_rows = student_weight.shape[0]
+    in_wave = (routes < owners).T
+    high = lax.reduce_precision(route_weights.T, 8, 7)
+    info = jnp.concatenate(
+        [jnp.where(in_wave, routes.T, -64), jnp.where(in_wave, slots.T, 0), high, route_weights.T - high]
+    ).astype(BF)
+    info = jnp.pad(info, ((0, 16), (0, student_weight.shape[1] - tokens)))
+    weight_info = jnp.concatenate([student_weight, info])
+    gathered = lax.all_gather(weight_info, "y", axis=0)
+
     slot_index = jnp.where(routes < owners, routes * CAP + slots, -1).T
     slot_ids = jnp.arange(slot_count, dtype=jnp.int32)[:, None]
     mask = jnp.zeros((slot_count, tokens), F32)
@@ -158,52 +223,57 @@
         mask = mask + (slot_index[k][None, :] == slot_ids).astype(F32)
     my_cols = lax.dynamic_slice_in_dim(teacher_tokens, (x * 2 + c) * width, width, 1)
     outgoing = jnp.dot(mask.astype(BF), my_cols, preferred_element_type=F32).astype(BF)
+    outgoing = after(outgoing, weight_info)
     arrived = lax.all_to_all(
         outgoing.reshape(owners, CAP, width), fsdp, split_axis=0, concat_axis=0, tiled=True
     ).reshape(slot_count, width)
 
-    projector_z = lax.all_gather(projector, "z", axis=0, tiled=True).reshape(
+    projector_z = lax.all_gather(after(projector, weight_info), "z", axis=0, tiled=True).reshape(
         zs, projector.shape[0], projector.shape[1]
     )
-    weight_y = [student_weight] + [shifted(student_weight, "y", hop) for hop in (1, 2, 3)]
-    weight_y = lax.dynamic_slice_in_dim(jnp.stack(weight_y * 2), (4 - y) % 4, 4, 0)
-    weight_y = weight_y.reshape(ys * student_weight.shape[0], student_weight.shape[1])
-    input_cols = student_input.shape[1] // zs
-    inputs_z = lax.all_to_all(
-        student_input.reshape(tokens, zs, input_cols).transpose(1, 0, 2),
-        "z",
-        split_axis=0,
-        concat_axis=0,
-        tiled=True,
-    ).reshape(zs * tokens, input_cols)
-    inputs_t = inputs_z.T
-    student_part = jnp.dot(inputs_z, weight_y, preferred_element_type=F32).astype(BF)
-    student_out = lax.psum_scatter(student_part, "z", scatter_dimension=0, tiled=True)
-
-    row_index = jnp.where(routes < owners, routes * (ys * CAP) + slots, -1).T
-    packed = jnp.concatenate([row_index.astype(F32), route_weights.T])
+    plans = gathered[:, weight_rows : weight_rows + 32, :tokens].astype(F32)
+    plans = lax.dynamic_slice_in_dim(jnp.concatenate([plans, plans]), y, ys, 0)
     combine_rows = []
     row_ids = jnp.arange(slot_count * ys, dtype=jnp.int32)[None, :]
     for hop in range(ys):
-        plan = packed if hop == 0 else shifted(packed, "y", hop)
-        base = ((y + hop) % ys) * CAP
+        plan = plans[hop]
+        place = plan[:8] * (ys * CAP) + plan[8:16] + (((y + hop) % ys) * CAP).astype(F32)
+        place, share = place.astype(jnp.int32), plan[16:24] + plan[24:32]
         part = jnp.zeros((tokens, slot_count * ys), F32)
         for k in range(8):
-            row = plan[k].astype(jnp.int32)
-            row = jnp.where(row >= 0, row + base, -1)
-            part = part + jnp.where(row[:, None] == row_ids, plan[8 + k][:, None], 0.0)
+            part = part + jnp.where(place[k][:, None] == row_ids, share[k][:, None], 0.0)
         combine_rows.append(part)
     combine = jnp.concatenate(combine_rows)
     combine_high = lax.reduce_precision(combine, 8, 7)
     combine_low = (combine - combine_high).astype(BF)
     combine_high = combine_high.astype(BF)
 
+    eight, four = jnp.arange(8, dtype=jnp.int32), jnp.arange(4, dtype=jnp.int32)
+    spots = jnp.where(eight < 5, eight, 4 - eight)
+    grad_order = jnp.concatenate([(z + spots) % zs, (y + four) % ys])
+    student_order = jnp.concatenate([jnp.stack([c, 1 - c]).astype(jnp.int32)])
+    tokens_half = tokens // 2
+    input_cols = student_input.shape[1] // zs
+    half = lax.dynamic_slice_in_dim(student_input, c * tokens_half, tokens_half, 0)
+    half = half.reshape(tokens_half, zs, input_cols).transpose(1, 0, 2)
+    arrived, order, grad_order, student_order, half = lax.optimization_barrier(
+        (arrived, order, grad_order, student_order, half)
+    )
+    half = lax.all_to_all(half, "z", split_axis=0, concat_axis=0, tiled=True)
+
     blocks = gather_expert(arrived)
     keep, send = ffn(order, blocks, gate_proj[0], up_proj[0], down_proj[0])
     taken = shifted(send, "c", 1)
     pairs = [(keep[i].astype(F32) + taken[i].astype(F32)).astype(BF) for i in range(4)]
     parts = [pairs[0]] + [shifted(pairs[hop], "x", -hop) for hop in (1, 2, 3)]
+    half = after(half, send)
+    other_half = shifted(half, "c", 1)
     outgoing_rows = fold(parts, zs, ys)
+    student_part, inputs_z = student(
+        after(student_order, outgoing_rows), [half, other_half], gathered
+    )
+    inputs_t = inputs_z.reshape(zs * tokens, input_cols).T
+    student_out = lax.psum_scatter(student_part, "z", scatter_dimension=0, tiled=True)
     returned = lax.all_to_all(
         outgoing_rows.reshape(owners, ys * CAP, width // ys),
         fsdp,
@@ -211,12 +281,15 @@
         concat_axis=0,
         tiled=True,
     ).reshape(slot_count * ys, width // ys)
+    returned, combine_high, combine_low = lax.optimization_barrier(
+        (returned, combine_high, combine_low, inputs_t)
+    )[:3]
     teacher = (
         jnp.dot(combine_high, returned, preferred_element_type=F32)
         + jnp.dot(combine_low, returned, preferred_element_type=F32)
     ).astype(BF)
 
-    sums = project(order, gather_expert(teacher), projector_z)
+    sums = project(order, gather_expert(after(teacher, projector_z)), projector_z)
     projected = sums[0]
     for hop in (1, 2, 3):
         projected = projected + shifted(sums[hop], "y", -hop).astype(F32)
@@ -229,8 +302,6 @@
         if hop < 4:
             behind.append(shifted(behind[-1], "z", -1))
     errors = [error] + ahead[1:] + behind[1:]
-    spots = jnp.array([0, 1, 2, 3, 4, -1, -2, -3], jnp.int32)
-    grad_order = jnp.concatenate([(z + spots) % zs, (y + jnp.arange(4, dtype=jnp.int32)) % ys])
     grads = gradient_parts(grad_order, errors, inputs_t)
     gradient = grads[0]
     for hop in (1, 2, 3):

time: 213 us -> 193 us (0.906)
  starting transfers between devices: 69.7 us -> 53.5 us
  local copies, waits for them, and re-layouts: 25.2 us -> 10.4 us
  waiting for transfers between devices: 80.3 us -> 87.8 us
  Pallas kernels: 9.67 us -> 13.1 us
  other arithmetic: 8.08 us -> 10.5 us
    ppermute x37 -> x32, waiting for transfers between devices: 50.6 us -> 69.4 us  [shifted(): lax.ppermute(value, axis, [(i, (i - hop) % size) for i in range(size)])]
    ppermute x37 -> x32, starting transfers between devices: 44.5 us -> 28.4 us  [shifted(): lax.ppermute(value, axis, [(i, (i - hop) % size) for i in range(size)])]
    all_to_all x1, waiting for transfers between devices: 13.2 us -> 0.01 us  [body(): half = lax.all_to_all(half, 'z', split_axis=0, concat_axis=0, tiled=True)]
    unnamed x50 -> x20, local copies, waits for them, and re-layouts: 19.4 us -> 6.21 us
    dot_general x1 -> x0, matrix products: 4.04 us -> none  [body(): jnp.dot(inputs_z, weight_y, preferred_element_type=F32).astype(BF)]
    all_to_all x1, waiting for transfers between devices: 4.77 us -> 8.74 us  [body(): lax.all_to_all(outgoing.reshape(owners, CAP, width), fsdp, split_axis=0,...]
    all_to_all x1, waiting for transfers between devices: 11.8 us -> 8.96 us  [body(): lax.all_to_all(outgoing_rows.reshape(owners, ys * CAP, width // ys), fsdp...]
    reshape x0 -> x2, local copies, waits for them, and re-layouts: none -> 2.52 us  [the longest x1 1.61 us: body(): inputs_t = inputs_z.reshape(zs * tokens, input_cols).T]
  transfers between devices with their start and end apart: 42 -> 38, of which waited for: 19 -> 23; matrix products, arithmetic and copies ran while one was open for 12% -> 6% of each run, Pallas kernels for 4% -> 6%
where the time goes in v2:
time: 193 us; the launch traced here: 192 us
  waiting for transfers between devices  87.8 us (45%)
  starting transfers between devices  53.5 us (28%)
  between operations  14.1 us (7%)
  Pallas kernels  13.1 us (7%)
  other arithmetic  10.5 us (5%)
  local copies, waits for them, and re-layouts  10.4 us (5%)
  matrix products  2.98 us (2%)
    ppermute x32, waiting for transfers between devices, shifted(): lax.ppermute(value, axis, [(i, (i - hop) % size) for i in range(size)])  69.4 us
    ppermute x32, starting transfers between devices, shifted(): lax.ppermute(value, axis, [(i, (i - hop) % size) for i in range(size)])  28.4 us
    all_to_all x1, starting transfers between devices, body(): lax.all_to_all(outgoing.reshape(owners, CAP, width), fsdp, split_axis=0,...  10.5 us
    all_to_all x1, waiting for transfers between devices, body(): lax.all_to_all(outgoing_rows.reshape(owners, ys * CAP, width // ys), fsdp...  8.96 us
    all_to_all x1, waiting for transfers between devices, body(): lax.all_to_all(outgoing.reshape(owners, CAP, width), fsdp, split_axis=0,...  8.74 us
    all_to_all x1, starting transfers between devices, body(): lax.all_to_all(outgoing_rows.reshape(owners, ys * CAP, width // ys), fsdp...  8.6 us
    unnamed x20, local copies, waits for them, and re-layouts  6.21 us
    all_to_all x1, starting transfers between devices, body(): half = lax.all_to_all(half, 'z', split_axis=0, concat_axis=0, tiled=True)  5.92 us
  transfers between devices with their start and end apart: 38, of which 23 were waited for; matrix products, arithmetic and copies ran while one was open for 6% of the time, Pallas kernels for 6%

profile of v2, /device:TPU:96, one launch (start us, length us, event | category | flops | bytes accessed | tf_op | source)
XLA Modules:
  0.0 192.3 jit_solution(13235575711402783440)
XLA Ops:
  12.3 10.5 %all-to-all-start = ((bf16[32,4,896]{2,1,0:T(4,128)(2,1)}), bf16[32,4,896]{2,1,0:T(4,128)(2,1)S(1)}, u32[]{:S(2)}, u32[]{:S(2)}) async-start(bf16[32,4,896]{2,1,0:T(4,128)(2,1)} %reshape.277), calls=%async_computation | async-start | bytes 458752 | tf_op jit(solution)/shard_map/all_to_all | solution.py:227
  24.0 8.7 %all-to-all-done = bf16[32,4,896]{2,1,0:T(4,128)(2,1)S(1)} async-done(((bf16[32,4,896]{2,1,0:T(4,128)(2,1)}), bf16[32,4,896]{2,1,0:T(4,128)(2,1)S(1)}, u32[]{:S(2)}, u32[]{:S(2)}) %all-to-all-start) | async-done | bytes 229408 | tf_op jit(solution)/shard_map/all_to_all | solution.py:227
  32.9 5.9 %all-to-all-start.2 = ((bf16[8,64,640]{2,1,0:T(8,128)(2,1)}), bf16[8,64,640]{2,1,0:T(8,128)(2,1)S(1)}, u32[]{:S(2)}, u32[]{:S(2)}) async-start(bf16[8,64,640]{2,1,0:T(8,128)(2,1)} %bitcast.182), calls=%async_computation.2 | async-start | bytes 1310720 | tf_op jit(solution)/shard_map/all_to_all | solution.py:262
  38.8 2.8 %collective-permute-start = (bf16[128,896]{1,0:T(8,128)(2,1)S(1)}, bf16[128,896]{1,0:T(8,128)(2,1)S(1)}, u32[]{:S(2)}, u32[]{:S(2)}) collective-permute-start(bf16[128,896]{1,0:T(8,128)(2,1)S(1)} %reshape.278.refs_0_), channel_id=1, source_target_pairs={{0,192},{64,0},{128,64},{192,128},{1,193},{65,1},{129,65},{193,129... | collective-permute-start | bytes 688136 | tf_op jit(solution)/shard_map/ppermute | solution.py:32
  43.2 6.0 %collective-permute-done.refs_1_ = bf16[128,896]{1,0:T(8,128)(2,1)S(1)} collective-permute-done((bf16[128,896]{1,0:T(8,128)(2,1)S(1)}, bf16[128,896]{1,0:T(8,128)(2,1)S(1)}, u32[]{:S(2)}, u32[]{:S(2)}) %collective-permute-start) | collective-permute-done | bytes 229408 | tf_op jit(solution)/shard_map/ppermute | solution.py:32
  55.4 5.4 %expert_ffn.1 = (bf16[4,128,896]{2,1,0:T(8,128)(2,1)S(1)}, bf16[4,128,896]{2,1,0:T(8,128)(2,1)}) custom-call(s32[8]{0:T(128)S(1)} %pad_add_fusion.order, bf16[128,896]{1,0:T(8,128)(2,1)S(1)} %copy-done.6, bf16[128,896]{1,0:T(8,128)(2,1)S(1)} %collective-permute-done.refs_1_, bf16[128,896]{1,0:T(8,128)(2,1)S(1)} %collective-permute-done.1.refs_2_, ...), custom_call_target="tpu_custom_call" | custom-call | tf_op jit(solution)/shard_map/expert_ffn/pallas_call | solution.py:77
  68.8 10.3 %collective-permute-done.8.b = bf16[128,896]{1,0:T(8,128)(2,1)S(1)} collective-permute-done((bf16[128,896]{1,0:T(8,128)(2,1)S(1)}, bf16[128,896]{1,0:T(8,128)(2,1)S(1)}, u32[]{:S(2)}, u32[]{:S(2)}) %collective-permute-start.8) | collective-permute-done | bytes 229408 | tf_op jit(solution)/shard_map/ppermute | solution.py:32
  80.7 2.5 %student.1 = (bf16[1024,640]{1,0:T(8,128)(2,1)S(1)}, bf16[8,128,640]{2,1,0:T(8,128)(2,1)S(1)}) custom-call(s32[2]{0:T(128)S(1)} %pad_add_fusion.2.order, bf16[8,64,640]{2,1,0:T(8,128)(2,1)S(1)} %all-to-all-done.2.refs_0_, bf16[8,64,640]{2,1,0:T(8,128)(2,1)} %collective-permute-done.11.refs_1_, bf16[4,208,640]{2,1,0:T(8,128)(2,1)S(1)} %bitcast.187), custom_call_target="tpu_custom_call" | custom-call | tf_op jit(solution)/shard_map/student/pallas_call | solution.py:173
  86.5 8.6 %all-to-all-start.1 = ((bf16[32,16,224]{2,1,0:T(8,128)(2,1)}), bf16[32,16,224]{2,1,0:T(8,128)(2,1)S(1)}, u32[]{:S(2)}, u32[]{:S(2)}) async-start(bf16[32,16,224]{2,1,0:T(8,128)(2,1)} %bitcast.22), calls=%async_computation.1 | async-start | bytes 524288 | tf_op jit(solution)/shard_map/all_to_all | solution.py:277
  98.2 9.0 %all-to-all-done.1 = bf16[32,16,224]{2,1,0:T(8,128)(2,1)S(1)} async-done(((bf16[32,16,224]{2,1,0:T(8,128)(2,1)}), bf16[32,16,224]{2,1,0:T(8,128)(2,1)S(1)}, u32[]{:S(2)}, u32[]{:S(2)}) %all-to-all-start.1) | async-done | bytes 229408 | tf_op jit(solution)/shard_map/all_to_all | solution.py:277
  110.7 3.1 %collective-permute-start.12 = (bf16[512,224]{1,0:T(8,128)(2,1)S(1)}, bf16[512,224]{1,0:T(8,128)(2,1)S(1)}, u32[]{:S(2)}, u32[]{:S(2)}) collective-permute-start(bf16[512,224]{1,0:T(8,128)(2,1)S(1)} %fusion.refs_0_), channel_id=1, source_target_pairs={{0,192},{64,0},{128,64},{192,128},{1,193},{65,1},{129,65},{193,129... | collective-permute-start | bytes 688136 | tf_op jit(solution)/shard_map/ppermute | solution.py:32
  114.7 6.9 %collective-permute-done.12.refs_1_ = bf16[512,224]{1,0:T(8,128)(2,1)S(1)} collective-permute-done((bf16[512,224]{1,0:T(8,128)(2,1)S(1)}, bf16[512,224]{1,0:T(8,128)(2,1)S(1)}, u32[]{:S(2)}, u32[]{:S(2)}) %collective-permute-start.12) | collective-permute-done | bytes 229408 | tf_op jit(solution)/shard_map/ppermute | solution.py:32
  122.7 2.4 %collective-permute-done.14.refs_3_ = bf16[512,224]{1,0:T(8,128)(2,1)S(1)} collective-permute-done((bf16[512,224]{1,0:T(8,128)(2,1)S(1)}, bf16[512,224]{1,0:T(8,128)(2,1)S(1)}, u32[]{:S(2)}, u32[]{:S(2)}) %collective-permute-start.14) | collective-permute-done | bytes 229408 | tf_op jit(solution)/shard_map/ppermute | solution.py:32
  135.0 3.5 %collective-permute-done.21 = bf16[128,640]{1,0:T(8,128)(2,1)S(1)} collective-permute-done((bf16[128,640]{1,0:T(8,128)(2,1)S(1)}, bf16[128,640]{1,0:T(8,128)(2,1)S(1)}, u32[]{:S(2)}, u32[]{:S(2)}) %collective-permute-start.21) | collective-permute-done | bytes 163872 | tf_op jit(solution)/shard_map/ppermute | solution.py:32
  138.5 3.3 %collective-permute-done.20 = bf16[128,640]{1,0:T(8,128)(2,1)S(1)} collective-permute-done((bf16[128,640]{1,0:T(8,128)(2,1)S(1)}, bf16[128,640]{1,0:T(8,128)(2,1)S(1)}, u32[]{:S(2)}, u32[]{:S(2)}) %collective-permute-start.20) | collective-permute-done | bytes 163872 | tf_op jit(solution)/shard_map/ppermute | solution.py:32
  141.7 2.4 %collective-permute-done.19 = bf16[128,640]{1,0:T(8,128)(2,1)} collective-permute-done((bf16[128,640]{1,0:T(8,128)(2,1)S(1)}, bf16[128,640]{1,0:T(8,128)(2,1)}, u32[]{:S(2)}, u32[]{:S(2)}) %collective-permute-start.19) | collective-permute-done | bytes 163872 | tf_op jit(solution)/shard_map/ppermute | solution.py:32
  146.3 3.0 %collective-permute-start.26 = (bf16[128,640]{1,0:T(8,128)(2,1)S(1)}, bf16[128,640]{1,0:T(8,128)(2,1)S(1)}, u32[]{:S(2)}, u32[]{:S(2)}) collective-permute-start(bf16[128,640]{1,0:T(8,128)(2,1)S(1)} %get-tuple-element.58.refs_0_), channel_id=1, source_target_pairs={{0,4},{4,8},{8,12},{12,16},{16,20},{20,24},{24,28},{28,0},{1,5},{5... | collective-permute-start | bytes 491528 | tf_op jit(solution)/shard_map/ppermute | solution.py:32
  149.3 4.1 %collective-permute-done.22.refs_1_ = bf16[128,640]{1,0:T(8,128)(2,1)S(1)} collective-permute-done((bf16[128,640]{1,0:T(8,128)(2,1)S(1)}, bf16[128,640]{1,0:T(8,128)(2,1)S(1)}, u32[]{:S(2)}, u32[]{:S(2)}) %collective-permute-start.22) | collective-permute-done | bytes 163872 | tf_op jit(solution)/shard_map/ppermute | solution.py:32
  153.4 3.2 %collective-permute-start.27 = (bf16[128,640]{1,0:T(8,128)(2,1)S(1)}, bf16[128,640]{1,0:T(8,128)(2,1)S(1)}, u32[]{:S(2)}, u32[]{:S(2)}) collective-permute-start(bf16[128,640]{1,0:T(8,128)(2,1)S(1)} %collective-permute-done.26.refs_5_), channel_id=1, source_target_pairs={{0,4},{4,8},{8,12},{12,16},{16,20},{20,24},{24,28},{28,0},{1,5},{5... | collective-permute-start | bytes 491528 | tf_op jit(solution)/shard_map/ppermute | solution.py:32
  156.7 3.3 %collective-permute-done.23.refs_2_ = bf16[128,640]{1,0:T(8,128)(2,1)S(1)} collective-permute-done((bf16[128,640]{1,0:T(8,128)(2,1)S(1)}, bf16[128,640]{1,0:T(8,128)(2,1)S(1)}, u32[]{:S(2)}, u32[]{:S(2)}) %collective-permute-start.23) | collective-permute-done | bytes 163872 | tf_op jit(solution)/shard_map/ppermute | solution.py:32
  159.9 3.2 %collective-permute-start.28 = (bf16[128,640]{1,0:T(8,128)(2,1)S(1)}, bf16[128,640]{1,0:T(8,128)(2,1)S(1)}, u32[]{:S(2)}, u32[]{:S(2)}) collective-permute-start(bf16[128,640]{1,0:T(8,128)(2,1)S(1)} %collective-permute-done.27.refs_6_), channel_id=1, source_target_pairs={{0,4},{4,8},{8,12},{12,16},{16,20},{20,24},{24,28},{28,0},{1,5},{5... | collective-permute-start | bytes 491528 | tf_op jit(solution)/shard_map/ppermute | solution.py:32
  163.2 3.3 %collective-permute-done.24.refs_3_ = bf16[128,640]{1,0:T(8,128)(2,1)S(1)} collective-permute-done((bf16[128,640]{1,0:T(8,128)(2,1)S(1)}, bf16[128,640]{1,0:T(8,128)(2,1)S(1)}, u32[]{:S(2)}, u32[]{:S(2)}) %collective-permute-start.24) | collective-permute-done | bytes 163872 | tf_op jit(solution)/shard_map/ppermute | solution.py:32
  166.5 6.5 %collective-permute-done.25.refs_4_ = bf16[128,640]{1,0:T(8,128)(2,1)S(1)} collective-permute-done((bf16[128,640]{1,0:T(8,128)(2,1)S(1)}, bf16[128,640]{1,0:T(8,128)(2,1)S(1)}, u32[]{:S(2)}, u32[]{:S(2)}) %collective-permute-start.25) | collective-permute-done | bytes 163872 | tf_op jit(solution)/shard_map/ppermute | solution.py:32
  177.5 3.3 %collective-permute-done.31 = bf16[160,640]{1,0:T(8,128)(2,1)S(1)} collective-permute-done((bf16[160,640]{1,0:T(8,128)(2,1)S(1)}, bf16[160,640]{1,0:T(8,128)(2,1)S(1)}, u32[]{:S(2)}, u32[]{:S(2)}) %collective-permute-start.31) | collective-permute-done | bytes 204832 | tf_op jit(solution)/shard_map/ppermute | solution.py:32
  (116 shorter events, 56.9 us)
Async XLA Ops:
  7.2 54.2 %all-gather.6.cloned.1.call-start = ((), (), s32[]{:S(2)}) async-start(), calls=%async_computation.6 | async-start | bytes 1331200 | tf_op jit(solution)/shard_map/all_gather | solution.py:217
  10.5 100.2 %all-gather.4.cloned.1.call-start = ((), (), s32[]{:S(2)}) async-start(), calls=%async_computation.4 | async-start | bytes 2580480 | tf_op jit(solution)/shard_map/all_gather | solution.py:231
  12.3 20.5 %all-to-all-start = ((bf16[32,4,896]{2,1,0:T(4,128)(2,1)}), bf16[32,4,896]{2,1,0:T(4,128)(2,1)S(1)}, u32[]{:S(2)}, u32[]{:S(2)}) async-start(bf16[32,4,896]{2,1,0:T(4,128)(2,1)} %reshape.277), calls=%async_computation | async-start | bytes 458752 | tf_op jit(solution)/shard_map/all_to_all | solution.py:227
  32.9 28.2 %all-to-all-start.2 = ((bf16[8,64,640]{2,1,0:T(8,128)(2,1)}), bf16[8,64,640]{2,1,0:T(8,128)(2,1)S(1)}, u32[]{:S(2)}, u32[]{:S(2)}) async-start(bf16[8,64,640]{2,1,0:T(8,128)(2,1)} %bitcast.182), calls=%async_computation.2 | async-start | bytes 1310720 | tf_op jit(solution)/shard_map/all_to_all | solution.py:262
  38.8 105.4 %reduce-scatter.2.cloned.1.call-start = ((), (), s32[]{:S(2)}) async-start(), calls=%async_computation.5 | async-start | bytes 1474560 | tf_op jit(solution)/shard_map/reduce_scatter | solution.py:276
  38.8 10.5 %collective-permute-start = (bf16[128,896]{1,0:T(8,128)(2,1)S(1)}, bf16[128,896]{1,0:T(8,128)(2,1)S(1)}, u32[]{:S(2)}, u32[]{:S(2)}) collective-permute-start(bf16[128,896]{1,0:T(8,128)(2,1)S(1)} %reshape.278.refs_0_), channel_id=1, source_target_pairs={{0,192},{64,0},{128,64},{192,128},{1,193},{65,1},{129,65},{193,129... | collective-permute-start | bytes 688136 | tf_op jit(solution)/shard_map/ppermute | solution.py:32
  41.5 9.1 %collective-permute-start.1 = (bf16[128,896]{1,0:T(8,128)(2,1)S(1)}, bf16[128,896]{1,0:T(8,128)(2,1)S(1)}, u32[]{:S(2)}, u32[]{:S(2)}) collective-permute-start(bf16[128,896]{1,0:T(8,128)(2,1)S(1)} %reshape.278.refs_0_), channel_id=1, source_target_pairs={{0,128},{64,192},{128,0},{192,64},{1,129},{65,193},{129,1},{193,65... | collective-permute-start | bytes 688136 | tf_op jit(solution)/shard_map/ppermute | solution.py:32
  42.3 10.6 %collective-permute-start.2 = (bf16[128,896]{1,0:T(8,128)(2,1)S(1)}, bf16[128,896]{1,0:T(8,128)(2,1)S(1)}, u32[]{:S(2)}, u32[]{:S(2)}) collective-permute-start(bf16[128,896]{1,0:T(8,128)(2,1)S(1)} %reshape.278.refs_0_), channel_id=1, source_target_pairs={{0,64},{64,128},{128,192},{192,0},{1,65},{65,129},{129,193},{193,1... | collective-permute-start | bytes 688136 | tf_op jit(solution)/shard_map/ppermute | solution.py:32
  43.2 9.8 %collective-permute-start.3 = (bf16[128,896]{1,0:T(8,128)(2,1)S(1)}, bf16[128,896]{1,0:T(8,128)(2,1)S(1)}, u32[]{:S(2)}, u32[]{:S(2)}) collective-permute-start(bf16[128,896]{1,0:T(8,128)(2,1)S(1)} %reshape.278.refs_0_), channel_id=1, source_target_pairs={{0,32},{32,0},{1,33},{33,1},{2,34},{34,2},{3,35},{35,3},{4,36},{36... | collective-permute-start | bytes 688136 | tf_op jit(solution)/shard_map/ppermute | solution.py:32
  61.0 19.7 %collective-permute-start.11 = (bf16[8,64,640]{2,1,0:T(8,128)(2,1)S(1)}, bf16[8,64,640]{2,1,0:T(8,128)(2,1)}, u32[]{:S(2)}, u32[]{:S(2)}) collective-permute-start(bf16[8,64,640]{2,1,0:T(8,128)(2,1)S(1)} %all-to-all-done.2.refs_0_), channel_id=1, source_target_pairs={{0,32},{32,0},{1,33},{33,1},{2,34},{34,2},{3,35},{35,3},{4,36},{36... | collective-permute-start | bytes 1966088 | tf_op jit(solution)/shard_map/ppermute | solution.py:32
  65.3 13.8 %collective-permute-start.8 = (bf16[128,896]{1,0:T(8,128)(2,1)S(1)}, bf16[128,896]{1,0:T(8,128)(2,1)S(1)}, u32[]{:S(2)}, u32[]{:S(2)}) collective-permute-start(bf16[128,896]{1,0:T(8,128)(2,1)S(1)} %get-tuple-element.54), channel_id=1, source_target_pairs={{0,64},{64,128},{128,192},{192,0},{1,65},{65,129},{129,193},{193,1... | collective-permute-start | bytes 688136 | tf_op jit(solution)/shard_map/ppermute | solution.py:32
  65.4 13.8 %collective-permute-start.9 = (bf16[128,896]{1,0:T(8,128)(2,1)S(1)}, bf16[128,896]{1,0:T(8,128)(2,1)S(1)}, u32[]{:S(2)}, u32[]{:S(2)}) collective-permute-start(bf16[128,896]{1,0:T(8,128)(2,1)S(1)} %get-tuple-element.53), channel_id=1, source_target_pairs={{0,128},{64,192},{128,0},{192,64},{1,129},{65,193},{129,1},{193,65... | collective-permute-start | bytes 688136 | tf_op jit(solution)/shard_map/ppermute | solution.py:32
  67.5 12.3 %collective-permute-start.10 = (bf16[128,896]{1,0:T(8,128)(2,1)S(1)}, bf16[128,896]{1,0:T(8,128)(2,1)S(1)}, u32[]{:S(2)}, u32[]{:S(2)}) collective-permute-start(bf16[128,896]{1,0:T(8,128)(2,1)S(1)} %get-tuple-element.52), channel_id=1, source_target_pairs={{0,192},{64,0},{128,64},{192,128},{1,193},{65,1},{129,65},{193,129... | collective-permute-start | bytes 688136 | tf_op jit(solution)/shard_map/ppermute | solution.py:32
  86.5 20.7 %all-to-all-start.1 = ((bf16[32,16,224]{2,1,0:T(8,128)(2,1)}), bf16[32,16,224]{2,1,0:T(8,128)(2,1)S(1)}, u32[]{:S(2)}, u32[]{:S(2)}) async-start(bf16[32,16,224]{2,1,0:T(8,128)(2,1)} %bitcast.22), calls=%async_computation.1 | async-start | bytes 524288 | tf_op jit(solution)/shard_map/all_to_all | solution.py:277
  110.7 11.0 %collective-permute-start.12 = (bf16[512,224]{1,0:T(8,128)(2,1)S(1)}, bf16[512,224]{1,0:T(8,128)(2,1)S(1)}, u32[]{:S(2)}, u32[]{:S(2)}) collective-permute-start(bf16[512,224]{1,0:T(8,128)(2,1)S(1)} %fusion.refs_0_), channel_id=1, source_target_pairs={{0,192},{64,0},{128,64},{192,128},{1,193},{65,1},{129,65},{193,129... | collective-permute-start | bytes 688136 | tf_op jit(solution)/shard_map/ppermute | solution.py:32
  113.8 9.0 %collective-permute-start.13 = (bf16[512,224]{1,0:T(8,128)(2,1)S(1)}, bf16[512,224]{1,0:T(8,128)(2,1)S(1)}, u32[]{:S(2)}, u32[]{:S(2)}) collective-permute-start(bf16[512,224]{1,0:T(8,128)(2,1)S(1)} %fusion.refs_0_), channel_id=1, source_target_pairs={{0,128},{64,192},{128,0},{192,64},{1,129},{65,193},{129,1},{193,65... | collective-permute-start | bytes 688136 | tf_op jit(solution)/shard_map/ppermute | solution.py:32
  113.8 11.4 %collective-permute-start.14 = (bf16[512,224]{1,0:T(8,128)(2,1)S(1)}, bf16[512,224]{1,0:T(8,128)(2,1)S(1)}, u32[]{:S(2)}, u32[]{:S(2)}) collective-permute-start(bf16[512,224]{1,0:T(8,128)(2,1)S(1)} %fusion.refs_0_), channel_id=1, source_target_pairs={{0,64},{64,128},{128,192},{192,0},{1,65},{65,129},{129,193},{193,1... | collective-permute-start | bytes 688136 | tf_op jit(solution)/shard_map/ppermute | solution.py:32
  114.7 10.4 %collective-permute-start.15 = (bf16[512,224]{1,0:T(8,128)(2,1)S(1)}, bf16[512,224]{1,0:T(8,128)(2,1)S(1)}, u32[]{:S(2)}, u32[]{:S(2)}) collective-permute-start(bf16[512,224]{1,0:T(8,128)(2,1)S(1)} %fusion.refs_0_), channel_id=1, source_target_pairs={{0,32},{32,0},{1,33},{33,1},{2,34},{34,2},{3,35},{35,3},{4,36},{36... | collective-permute-start | bytes 688136 | tf_op jit(solution)/shard_map/ppermute | solution.py:32
  133.1 8.6 %collective-permute-start.20 = (bf16[128,640]{1,0:T(8,128)(2,1)S(1)}, bf16[128,640]{1,0:T(8,128)(2,1)S(1)}, u32[]{:S(2)}, u32[]{:S(2)}) collective-permute-start(bf16[128,640]{1,0:T(8,128)(2,1)S(1)} %get-tuple-element.44), channel_id=1, source_target_pairs={{0,2},{1,3},{2,0},{3,1},{4,6},{5,7},{6,4},{7,5},{8,10},{9,11},{10,... | collective-permute-start | bytes 491528 | tf_op jit(solution)/shard_map/ppermute | solution.py:32
  134.2 10.0 %collective-permute-start.19 = (bf16[128,640]{1,0:T(8,128)(2,1)S(1)}, bf16[128,640]{1,0:T(8,128)(2,1)}, u32[]{:S(2)}, u32[]{:S(2)}) collective-permute-start(bf16[128,640]{1,0:T(8,128)(2,1)S(1)} %get-tuple-element.43), channel_id=1, source_target_pairs={{0,1},{1,2},{2,3},{3,0},{4,5},{5,6},{6,7},{7,4},{8,9},{9,10},{10,1... | collective-permute-start | bytes 491528 | tf_op jit(solution)/shard_map/ppermute | solution.py:32
  146.1 7.3 %collective-permute-start.22 = (bf16[128,640]{1,0:T(8,128)(2,1)S(1)}, bf16[128,640]{1,0:T(8,128)(2,1)S(1)}, u32[]{:S(2)}, u32[]{:S(2)}) collective-permute-start(bf16[128,640]{1,0:T(8,128)(2,1)S(1)} %get-tuple-element.58.refs_0_), channel_id=1, source_target_pairs={{0,28},{4,0},{8,4},{12,8},{16,12},{20,16},{24,20},{28,24},{1,29},{... | collective-permute-start | bytes 491528 | tf_op jit(solution)/shard_map/ppermute | solution.py:32
  146.3 7.2 %collective-permute-start.26 = (bf16[128,640]{1,0:T(8,128)(2,1)S(1)}, bf16[128,640]{1,0:T(8,128)(2,1)S(1)}, u32[]{:S(2)}, u32[]{:S(2)}) collective-permute-start(bf16[128,640]{1,0:T(8,128)(2,1)S(1)} %get-tuple-element.58.refs_0_), channel_id=1, source_target_pairs={{0,4},{4,8},{8,12},{12,16},{16,20},{20,24},{24,28},{28,0},{1,5},{5... | collective-permute-start | bytes 491528 | tf_op jit(solution)/shard_map/ppermute | solution.py:32
  175.5 7.4 %collective-permute-start.30 = (bf16[160,640]{1,0:T(8,128)(2,1)S(1)}, bf16[160,640]{1,0:T(8,128)(2,1)S(1)}, u32[]{:S(2)}, u32[]{:S(2)}) collective-permute-start(bf16[160,640]{1,0:T(8,128)(2,1)S(1)} %get-tuple-element.50), channel_id=1, source_target_pairs={{0,2},{1,3},{2,0},{3,1},{4,6},{5,7},{6,4},{7,5},{8,10},{9,11},{10,... | collective-permute-start | bytes 614408 | tf_op jit(solution)/shard_map/ppermute | solution.py:32
  176.5 8.4 %collective-permute-start.29 = (bf16[160,640]{1,0:T(8,128)(2,1)S(1)}, bf16[160,640]{1,0:T(8,128)(2,1)S(1)}, u32[]{:S(2)}, u32[]{:S(2)}) collective-permute-start(bf16[160,640]{1,0:T(8,128)(2,1)S(1)} %get-tuple-element.49), channel_id=1, source_target_pairs={{0,1},{1,2},{2,3},{3,0},{4,5},{5,6},{6,7},{7,4},{8,9},{9,10},{10,1... | collective-permute-start | bytes 614408 | tf_op jit(solution)/shard_map/ppermute | solution.py:32
  (24 other events, 128.1 us)
Sparse Core Ops, SparseCore 0:
  10.7 29.3 all-gather.5
  41.9 41.1 all-gather.3
  85.6 41.2 reduce-scatter.1

commit v3 on v2

--- a/solution.py
+++ b/solution.py
@@ -39,27 +39,30 @@
 
 
 def ffn_kernel(order, *refs):
-    blocks, hbm, (keep, send), (gate, up, down, sems) = refs[:8], refs[8:11], refs[11:13], refs[13:]
+    blocks, hbm, (keep, send), (both, down, sems) = refs[:8], refs[8:11], refs[11:13], refs[13:]
     width = blocks[0].shape[1]
+    hidden_units = down.shape[0]
 
     def rows(k):
         return pl.ds(pl.multiple_of(order[k] * width, 128), width)
 
     copies = [
-        pltpu.make_async_copy(hbm[i].at[rows(k), :], target.at[rows(k), :], sems.at[2 * k + i])
+        pltpu.make_async_copy(
+            hbm[i].at[rows(k), :],
+            both.at[rows(k), pl.ds(i * hidden_units, hidden_units)],
+            sems.at[2 * k + i],
+        )
         for k in range(8)
-        for i, target in enumerate((gate, up))
+        for i in range(2)
     ] + [pltpu.make_async_copy(hbm[2], down, sems.at[16])]
     for copy in copies:
         copy.start()
-    gate_act = jnp.zeros((blocks[0].shape[0], gate.shape[1]), F32)
-    up_act = jnp.zeros_like(gate_act)
+    acts = jnp.zeros((blocks[0].shape[0], 2 * hidden_units), F32)
     for k in range(8):
         copies[2 * k].wait()
         copies[2 * k + 1].wait()
-        block = blocks[k][...]
-        gate_act += jnp.dot(block, gate[rows(k), :], preferred_element_type=F32)
-        up_act += jnp.dot(block, up[rows(k), :], preferred_element_type=F32)
+        acts += jnp.dot(blocks[k][...], both[rows(k), :], preferred_element_type=F32)
+    gate_act, up_act = acts[:, :hidden_units], acts[:, hidden_units:]
     copies[16].wait()
     hidden = (gate_act / (1.0 + jnp.exp(-gate_act)) * up_act).astype(BF)
     for k in (4, 5, 6, 7, 0, 1, 2, 3):
@@ -79,7 +82,7 @@
         out_shape=(shape, shape),
         in_specs=[SMEM] + [VMEM] * 8 + [pl.BlockSpec(memory_space=pltpu.HBM)] * 3,
         out_specs=(VMEM, VMEM),
-        scratch_shapes=[pltpu.VMEM(weight.shape, BF) for weight in (gate, up, down)]
+        scratch_shapes=[pltpu.VMEM((gate.shape[0], 2 * gate.shape[1]), BF), pltpu.VMEM(down.shape, BF)]
         + [pltpu.SemaphoreType.DMA((17,))],
         compiler_params=limit(16),
         name="expert_ffn",
@@ -104,6 +107,24 @@
         compiler_params=limit(8),
         name="sum_and_split",
     )(*parts)
+
+
+def load_kernel(source, target, sem):
+    copy = pltpu.make_async_copy(source, target, sem)
+    copy.start()
+    copy.wait()
+
+
+def load(value):
+    return pl.pallas_call(
+        load_kernel,
+        out_shape=pltpu.VMEM(value.shape, value.dtype),
+        in_specs=[pl.BlockSpec(memory_space=pltpu.HBM)],
+        out_specs=VMEM,
+        scratch_shapes=[pltpu.SemaphoreType.DMA],
+        compiler_params=limit(4),
+        name="load",
+    )(in_hbm(value))
 
 
 def project_kernel(order, *refs):
@@ -156,29 +177,34 @@
 
 
 def student_kernel(order, *refs):
-    halves, gathered, part, inputs, weight = refs[:2], refs[2], refs[3], refs[4], refs[5]
+    halves, gathered, outs, (part, inputs, weight, sems) = refs[:2], refs[2], refs[3:5], refs[5:]
     tokens = halves[0].shape[1]
     for k in range(2):
         inputs[:, pl.ds(pl.multiple_of(order[k] * tokens, 32), tokens), :] = halves[k][...]
+    keep_inputs = pltpu.make_async_copy(inputs, outs[1], sems.at[0])
+    keep_inputs.start()
     rows = weight.shape[0] // 4
     for k in range(4):
         weight[k * rows : (k + 1) * rows, :] = gathered[k, :rows, :]
     flat = inputs[...].reshape(part.shape[0], weight.shape[0])
     part[...] = jnp.dot(flat, weight[...], preferred_element_type=F32).astype(BF)
+    keep_part = pltpu.make_async_copy(part, outs[0], sems.at[1])
+    keep_part.start()
+    keep_inputs.wait()
+    keep_part.wait()
 
 
 def student(order, halves, gathered):
     zs, tokens, width = halves[0].shape
     cols = gathered.shape[2]
+    shapes = ((zs * 2 * tokens, cols), (zs, 2 * tokens, width))
     return pl.pallas_call(
         student_kernel,
-        out_shape=(
-            jax.ShapeDtypeStruct((zs * 2 * tokens, cols), BF),
-            jax.ShapeDtypeStruct((zs, 2 * tokens, width), BF),
-        ),
+        out_shape=tuple(pltpu.HBM(shape, BF) for shape in shapes),
         in_specs=[SMEM] + [VMEM] * 3,
-        out_specs=(VMEM, VMEM),
-        scratch_shapes=[pltpu.VMEM((width, cols), BF)],
+        out_specs=(pl.BlockSpec(memory_space=pltpu.HBM),) * 2,
+        scratch_shapes=[pltpu.VMEM(shape, BF) for shape in shapes]
+        + [pltpu.VMEM((width, cols), BF), pltpu.SemaphoreType.DMA((2,))],
         compiler_params=limit(16),
         name="student",
     )(order, *halves, gathered)
@@ -244,9 +270,7 @@
             part = part + jnp.where(place[k][:, None] == row_ids, share[k][:, None], 0.0)
         combine_rows.append(part)
     combine = jnp.concatenate(combine_rows)
-    combine_high = lax.reduce_precision(combine, 8, 7)
-    combine_low = (combine - combine_high).astype(BF)
-    combine_high = combine_high.astype(BF)
+    combine = combine.astype(BF)
 
     eight, four = jnp.arange(8, dtype=jnp.int32), jnp.arange(4, dtype=jnp.int32)
     spots = jnp.where(eight < 5, eight, 4 - eight)
@@ -281,15 +305,11 @@
         concat_axis=0,
         tiled=True,
     ).reshape(slot_count * ys, width // ys)
-    returned, combine_high, combine_low = lax.optimization_barrier(
-        (returned, combine_high, combine_low, inputs_t)
-    )[:3]
-    teacher = (
-        jnp.dot(combine_high, returned, preferred_element_type=F32)
-        + jnp.dot(combine_low, returned, preferred_element_type=F32)
-    ).astype(BF)
-
-    sums = project(order, gather_expert(after(teacher, projector_z)), projector_z)
+    returned, combine = lax.optimization_barrier((returned, combine, inputs_t))[:2]
+    teacher = jnp.dot(combine, returned, preferred_element_type=F32).astype(BF)
+
+    teacher = after(teacher, projector_z)
+    sums = project(order, gather_expert(teacher), load(after(projector_z, teacher)))
     projected = sums[0]
     for hop in (1, 2, 3):
         projected = projected + shifted(sums[hop], "y", -hop).astype(F32)

time: 193 us -> 186 us (0.964)
  waiting for transfers between devices: 87.8 us -> 81.6 us
  local copies, waits for them, and re-layouts: 10.4 us -> 6.58 us
  Pallas kernels: 13.1 us -> 15.8 us
    ppermute x32, waiting for transfers between devices: 69.4 us -> 65.2 us  [shifted(): lax.ppermute(value, axis, [(i, (i - hop) % size) for i in range(size)])]
    unnamed x20 -> x14, local copies, waits for them, and re-layouts: 6.21 us -> 2.38 us
    pallas_call x1 -> x2, Pallas kernels: 2.52 us -> 5.34 us  [the longest x1 3.67 us: student(): pl.pallas_call(student_kernel, out_shape=tuple((pltpu.HBM(shape, BF) for...]
    all_to_all x1, waiting for transfers between devices: 8.96 us -> 6.92 us  [body(): lax.all_to_all(outgoing_rows.reshape(owners, ys * CAP, width // ys), fsdp...]
  transfers between devices with their start and end apart: 38 -> 38, of which waited for: 23 -> 20; matrix products, arithmetic and copies ran while one was open for 6% -> 5% of each run, Pallas kernels for 6% -> 8%
where the time goes in v3:
time: 186 us; the launch traced here: 185 us
  waiting for transfers between devices  81.6 us (44%)
  starting transfers between devices  55.1 us (30%)
  Pallas kernels  15.8 us (8%)
  between operations  14.1 us (8%)
  other arithmetic  10.2 us (5%)
  local copies, waits for them, and re-layouts  6.58 us (4%)
    ppermute x32, waiting for transfers between devices, shifted(): lax.ppermute(value, axis, [(i, (i - hop) % size) for i in range(size)])  65.2 us
    ppermute x32, starting transfers between devices, shifted(): lax.ppermute(value, axis, [(i, (i - hop) % size) for i in range(size)])  30 us
    all_to_all x1, starting transfers between devices, body(): lax.all_to_all(outgoing.reshape(owners, CAP, width), fsdp, split_axis=0,...  10.5 us
    all_to_all x1, waiting for transfers between devices, body(): lax.all_to_all(outgoing.reshape(owners, CAP, width), fsdp, split_axis=0,...  8.74 us
    all_to_all x1, starting transfers between devices, body(): lax.all_to_all(outgoing_rows.reshape(owners, ys * CAP, width // ys), fsdp...  8.65 us
    all_to_all x1, waiting for transfers between devices, body(): lax.all_to_all(outgoing_rows.reshape(owners, ys * CAP, width // ys), fsdp...  6.92 us
    all_to_all x1, starting transfers between devices, body(): half = lax.all_to_all(half, 'z', split_axis=0, concat_axis=0, tiled=True)  5.92 us
    pallas_call x1, Pallas kernels, ffn(): pl.pallas_call(ffn_kernel, out_shape=(shape, shape), in_specs=[SMEM] + [V...  5.3 us
  transfers between devices with their start and end apart: 38, of which 20 were waited for; matrix products, arithmetic and copies ran while one was open for 5% of the time, Pallas kernels for 8%

profile of v3, /device:TPU:96, one launch (start us, length us, event | category | flops | bytes accessed | tf_op | source)
XLA Modules:
  0.0 185.0 jit_solution(13982344945949108574)
XLA Ops:
  12.3 10.5 %all-to-all-start = ((bf16[32,4,896]{2,1,0:T(4,128)(2,1)}), bf16[32,4,896]{2,1,0:T(4,128)(2,1)S(1)}, u32[]{:S(2)}, u32[]{:S(2)}) async-start(bf16[32,4,896]{2,1,0:T(4,128)(2,1)} %reshape.277), calls=%async_computation | async-start | bytes 458752 | tf_op jit(solution)/shard_map/all_to_all | solution.py:253
  24.0 8.7 %all-to-all-done = bf16[32,4,896]{2,1,0:T(4,128)(2,1)S(1)} async-done(((bf16[32,4,896]{2,1,0:T(4,128)(2,1)}), bf16[32,4,896]{2,1,0:T(4,128)(2,1)S(1)}, u32[]{:S(2)}, u32[]{:S(2)}) %all-to-all-start) | async-done | bytes 229408 | tf_op jit(solution)/shard_map/all_to_all | solution.py:253
  32.9 5.9 %all-to-all-start.2 = ((bf16[8,64,640]{2,1,0:T(8,128)(2,1)}), bf16[8,64,640]{2,1,0:T(8,128)(2,1)S(1)}, u32[]{:S(2)}, u32[]{:S(2)}) async-start(bf16[8,64,640]{2,1,0:T(8,128)(2,1)} %bitcast.180), calls=%async_computation.2 | async-start | bytes 1310720 | tf_op jit(solution)/shard_map/all_to_all | solution.py:286
  38.8 2.8 %collective-permute-start = (bf16[128,896]{1,0:T(8,128)(2,1)S(1)}, bf16[128,896]{1,0:T(8,128)(2,1)S(1)}, u32[]{:S(2)}, u32[]{:S(2)}) collective-permute-start(bf16[128,896]{1,0:T(8,128)(2,1)S(1)} %reshape.278.refs_0_), channel_id=1, source_target_pairs={{0,192},{64,0},{128,64},{192,128},{1,193},{65,1},{129,65},{193,129... | collective-permute-start | bytes 688136 | tf_op jit(solution)/shard_map/ppermute | solution.py:32
  43.2 6.0 %collective-permute-done.refs_1_ = bf16[128,896]{1,0:T(8,128)(2,1)S(1)} collective-permute-done((bf16[128,896]{1,0:T(8,128)(2,1)S(1)}, bf16[128,896]{1,0:T(8,128)(2,1)S(1)}, u32[]{:S(2)}, u32[]{:S(2)}) %collective-permute-start) | collective-permute-done | bytes 229408 | tf_op jit(solution)/shard_map/ppermute | solution.py:32
  55.4 5.3 %expert_ffn.1 = (bf16[4,128,896]{2,1,0:T(8,128)(2,1)S(1)}, bf16[4,128,896]{2,1,0:T(8,128)(2,1)}) custom-call(s32[8]{0:T(128)S(1)} %pad_add_fusion.order, bf16[128,896]{1,0:T(8,128)(2,1)S(1)} %copy-done.3, bf16[128,896]{1,0:T(8,128)(2,1)S(1)} %collective-permute-done.refs_1_, bf16[128,896]{1,0:T(8,128)(2,1)S(1)} %collective-permute-done.1.refs_2_, ...), custom_call_target="tpu_custom_call" | custom-call | tf_op jit(solution)/shard_map/expert_ffn/pallas_call | solution.py:80
  68.1 5.6 %collective-permute-done.10.d = bf16[128,896]{1,0:T(8,128)(2,1)S(1)} collective-permute-done((bf16[128,896]{1,0:T(8,128)(2,1)S(1)}, bf16[128,896]{1,0:T(8,128)(2,1)S(1)}, u32[]{:S(2)}, u32[]{:S(2)}) %collective-permute-start.10) | collective-permute-done | bytes 229408 | tf_op jit(solution)/shard_map/ppermute | solution.py:32
  73.8 5.7 %collective-permute-done.8.b = bf16[128,896]{1,0:T(8,128)(2,1)S(1)} collective-permute-done((bf16[128,896]{1,0:T(8,128)(2,1)S(1)}, bf16[128,896]{1,0:T(8,128)(2,1)S(1)}, u32[]{:S(2)}, u32[]{:S(2)}) %collective-permute-start.8) | collective-permute-done | bytes 229408 | tf_op jit(solution)/shard_map/ppermute | solution.py:32
  80.4 3.7 %student.1 = (bf16[1024,640]{1,0:T(8,128)(2,1)}, bf16[8,128,640]{2,1,0:T(8,128)(2,1)}) custom-call(s32[2]{0:T(128)S(1)} %pad_add_fusion.2.order, bf16[8,64,640]{2,1,0:T(8,128)(2,1)S(1)} %all-to-all-done.2.refs_0_, bf16[8,64,640]{2,1,0:T(8,128)(2,1)} %collective-permute-done.11.refs_1_, bf16[4,208,640]{2,1,0:T(8,128)(2,1)S(1)} %bitcast.183), custom_call_target="tpu_custom_call" | custom-call | tf_op jit(solution)/shard_map/student/pallas_call | solution.py:201
  85.2 8.7 %all-to-all-start.1 = ((bf16[32,16,224]{2,1,0:T(8,128)(2,1)}), bf16[32,16,224]{2,1,0:T(8,128)(2,1)S(1)}, u32[]{:S(2)}, u32[]{:S(2)}) async-start(bf16[32,16,224]{2,1,0:T(8,128)(2,1)} %bitcast.22), calls=%async_computation.1 | async-start | bytes 524288 | tf_op jit(solution)/shard_map/all_to_all | solution.py:301
  96.7 6.9 %all-to-all-done.1 = bf16[32,16,224]{2,1,0:T(8,128)(2,1)S(1)} async-done(((bf16[32,16,224]{2,1,0:T(8,128)(2,1)}), bf16[32,16,224]{2,1,0:T(8,128)(2,1)S(1)}, u32[]{:S(2)}, u32[]{:S(2)}) %all-to-all-start.1) | async-done | bytes 229408 | tf_op jit(solution)/shard_map/all_to_all | solution.py:301
  108.9 7.6 %collective-permute-done.12.refs_1_ = bf16[512,224]{1,0:T(8,128)(2,1)S(1)} collective-permute-done((bf16[512,224]{1,0:T(8,128)(2,1)S(1)}, bf16[512,224]{1,0:T(8,128)(2,1)S(1)}, u32[]{:S(2)}, u32[]{:S(2)}) %collective-permute-start.12) | collective-permute-done | bytes 229408 | tf_op jit(solution)/shard_map/ppermute | solution.py:32
  117.4 2.4 %collective-permute-done.14.refs_3_ = bf16[512,224]{1,0:T(8,128)(2,1)S(1)} collective-permute-done((bf16[512,224]{1,0:T(8,128)(2,1)S(1)}, bf16[512,224]{1,0:T(8,128)(2,1)S(1)}, u32[]{:S(2)}, u32[]{:S(2)}) %collective-permute-start.14) | collective-permute-done | bytes 229408 | tf_op jit(solution)/shard_map/ppermute | solution.py:32
  125.0 2.5 %collective-permute-start.20 = (bf16[128,640]{1,0:T(8,128)(2,1)S(1)}, bf16[128,640]{1,0:T(8,128)(2,1)S(1)}, u32[]{:S(2)}, u32[]{:S(2)}) collective-permute-start(bf16[128,640]{1,0:T(8,128)(2,1)S(1)} %get-tuple-element.44), channel_id=1, source_target_pairs={{0,2},{1,3},{2,0},{3,1},{4,6},{5,7},{6,4},{7,5},{8,10},{9,11},{10,... | collective-permute-start | bytes 491528 | tf_op jit(solution)/shard_map/ppermute | solution.py:32
  129.1 6.9 %collective-permute-done.19 = bf16[128,640]{1,0:T(8,128)(2,1)S(1)} collective-permute-done((bf16[128,640]{1,0:T(8,128)(2,1)S(1)}, bf16[128,640]{1,0:T(8,128)(2,1)S(1)}, u32[]{:S(2)}, u32[]{:S(2)}) %collective-permute-start.19) | collective-permute-done | bytes 163872 | tf_op jit(solution)/shard_map/ppermute | solution.py:32
  141.9 3.5 %collective-permute-done.22.refs_1_ = bf16[128,640]{1,0:T(8,128)(2,1)S(1)} collective-permute-done((bf16[128,640]{1,0:T(8,128)(2,1)S(1)}, bf16[128,640]{1,0:T(8,128)(2,1)S(1)}, u32[]{:S(2)}, u32[]{:S(2)}) %collective-permute-start.22) | collective-permute-done | bytes 163872 | tf_op jit(solution)/shard_map/ppermute | solution.py:32
  145.5 3.2 %collective-permute-start.27 = (bf16[128,640]{1,0:T(8,128)(2,1)S(1)}, bf16[128,640]{1,0:T(8,128)(2,1)S(1)}, u32[]{:S(2)}, u32[]{:S(2)}) collective-permute-start(bf16[128,640]{1,0:T(8,128)(2,1)S(1)} %collective-permute-done.26.refs_5_), channel_id=1, source_target_pairs={{0,4},{4,8},{8,12},{12,16},{16,20},{20,24},{24,28},{28,0},{1,5},{5... | collective-permute-start | bytes 491528 | tf_op jit(solution)/shard_map/ppermute | solution.py:32
  148.7 3.3 %collective-permute-done.23.refs_2_ = bf16[128,640]{1,0:T(8,128)(2,1)S(1)} collective-permute-done((bf16[128,640]{1,0:T(8,128)(2,1)S(1)}, bf16[128,640]{1,0:T(8,128)(2,1)S(1)}, u32[]{:S(2)}, u32[]{:S(2)}) %collective-permute-start.23) | collective-permute-done | bytes 163872 | tf_op jit(solution)/shard_map/ppermute | solution.py:32
  151.9 3.2 %collective-permute-start.28 = (bf16[128,640]{1,0:T(8,128)(2,1)S(1)}, bf16[128,640]{1,0:T(8,128)(2,1)S(1)}, u32[]{:S(2)}, u32[]{:S(2)}) collective-permute-start(bf16[128,640]{1,0:T(8,128)(2,1)S(1)} %collective-permute-done.27.refs_6_), channel_id=1, source_target_pairs={{0,4},{4,8},{8,12},{12,16},{16,20},{20,24},{24,28},{28,0},{1,5},{5... | collective-permute-start | bytes 491528 | tf_op jit(solution)/shard_map/ppermute | solution.py:32
  155.2 3.3 %collective-permute-done.24.refs_3_ = bf16[128,640]{1,0:T(8,128)(2,1)S(1)} collective-permute-done((bf16[128,640]{1,0:T(8,128)(2,1)S(1)}, bf16[128,640]{1,0:T(8,128)(2,1)S(1)}, u32[]{:S(2)}, u32[]{:S(2)}) %collective-permute-start.24) | collective-permute-done | bytes 163872 | tf_op jit(solution)/shard_map/ppermute | solution.py:32
  158.5 6.5 %collective-permute-done.25.refs_4_ = bf16[128,640]{1,0:T(8,128)(2,1)S(1)} collective-permute-done((bf16[128,640]{1,0:T(8,128)(2,1)S(1)}, bf16[128,640]{1,0:T(8,128)(2,1)S(1)}, u32[]{:S(2)}, u32[]{:S(2)}) %collective-permute-start.25) | collective-permute-done | bytes 163872 | tf_op jit(solution)/shard_map/ppermute | solution.py:32
  168.8 2.9 %collective-permute-start.30 = (bf16[160,640]{1,0:T(8,128)(2,1)S(1)}, bf16[160,640]{1,0:T(8,128)(2,1)S(1)}, u32[]{:S(2)}, u32[]{:S(2)}) collective-permute-start(bf16[160,640]{1,0:T(8,128)(2,1)S(1)} %get-tuple-element.50), channel_id=1, source_target_pairs={{0,2},{1,3},{2,0},{3,1},{4,6},{5,7},{6,4},{7,5},{8,10},{9,11},{10,... | collective-permute-start | bytes 614408 | tf_op jit(solution)/shard_map/ppermute | solution.py:32
  171.7 2.9 %collective-permute-done.29 = bf16[160,640]{1,0:T(8,128)(2,1)S(1)} collective-permute-done((bf16[160,640]{1,0:T(8,128)(2,1)S(1)}, bf16[160,640]{1,0:T(8,128)(2,1)S(1)}, u32[]{:S(2)}, u32[]{:S(2)}) %collective-permute-start.29) | collective-permute-done | bytes 204832 | tf_op jit(solution)/shard_map/ppermute | solution.py:32
  174.6 3.0 %collective-permute-done.30 = bf16[160,640]{1,0:T(8,128)(2,1)S(1)} collective-permute-done((bf16[160,640]{1,0:T(8,128)(2,1)S(1)}, bf16[160,640]{1,0:T(8,128)(2,1)S(1)}, u32[]{:S(2)}, u32[]{:S(2)}) %collective-permute-start.30) | collective-permute-done | bytes 204832 | tf_op jit(solution)/shard_map/ppermute | solution.py:32
  (110 shorter events, 49.9 us)
Async XLA Ops:
  7.2 54.1 %all-gather.6.cloned.1.call-start = ((), (), s32[]{:S(2)}) async-start(), calls=%async_computation.6 | async-start | bytes 1331200 | tf_op jit(solution)/shard_map/all_gather | solution.py:243
  10.5 95.2 %all-gather.4.cloned.1.call-start = ((), (), s32[]{:S(2)}) async-start(), calls=%async_computation.4 | async-start | bytes 2580480 | tf_op jit(solution)/shard_map/all_gather | solution.py:257
  12.3 20.5 %all-to-all-start = ((bf16[32,4,896]{2,1,0:T(4,128)(2,1)}), bf16[32,4,896]{2,1,0:T(4,128)(2,1)S(1)}, u32[]{:S(2)}, u32[]{:S(2)}) async-start(bf16[32,4,896]{2,1,0:T(4,128)(2,1)} %reshape.277), calls=%async_computation | async-start | bytes 458752 | tf_op jit(solution)/shard_map/all_to_all | solution.py:253
  32.9 28.1 %all-to-all-start.2 = ((bf16[8,64,640]{2,1,0:T(8,128)(2,1)}), bf16[8,64,640]{2,1,0:T(8,128)(2,1)S(1)}, u32[]{:S(2)}, u32[]{:S(2)}) async-start(bf16[8,64,640]{2,1,0:T(8,128)(2,1)} %bitcast.180), calls=%async_computation.2 | async-start | bytes 1310720 | tf_op jit(solution)/shard_map/all_to_all | solution.py:286
  38.8 98.0 %reduce-scatter.2.cloned.1.call-start = ((), (), s32[]{:S(2)}) async-start(), calls=%async_computation.5 | async-start | bytes 1474560 | tf_op jit(solution)/shard_map/reduce_scatter | solution.py:300
  38.8 10.5 %collective-permute-start = (bf16[128,896]{1,0:T(8,128)(2,1)S(1)}, bf16[128,896]{1,0:T(8,128)(2,1)S(1)}, u32[]{:S(2)}, u32[]{:S(2)}) collective-permute-start(bf16[128,896]{1,0:T(8,128)(2,1)S(1)} %reshape.278.refs_0_), channel_id=1, source_target_pairs={{0,192},{64,0},{128,64},{192,128},{1,193},{65,1},{129,65},{193,129... | collective-permute-start | bytes 688136 | tf_op jit(solution)/shard_map/ppermute | solution.py:32
  41.5 9.1 %collective-permute-start.1 = (bf16[128,896]{1,0:T(8,128)(2,1)S(1)}, bf16[128,896]{1,0:T(8,128)(2,1)S(1)}, u32[]{:S(2)}, u32[]{:S(2)}) collective-permute-start(bf16[128,896]{1,0:T(8,128)(2,1)S(1)} %reshape.278.refs_0_), channel_id=1, source_target_pairs={{0,128},{64,192},{128,0},{192,64},{1,129},{65,193},{129,1},{193,65... | collective-permute-start | bytes 688136 | tf_op jit(solution)/shard_map/ppermute | solution.py:32
  42.3 10.6 %collective-permute-start.2 = (bf16[128,896]{1,0:T(8,128)(2,1)S(1)}, bf16[128,896]{1,0:T(8,128)(2,1)S(1)}, u32[]{:S(2)}, u32[]{:S(2)}) collective-permute-start(bf16[128,896]{1,0:T(8,128)(2,1)S(1)} %reshape.278.refs_0_), channel_id=1, source_target_pairs={{0,64},{64,128},{128,192},{192,0},{1,65},{65,129},{129,193},{193,1... | collective-permute-start | bytes 688136 | tf_op jit(solution)/shard_map/ppermute | solution.py:32
  43.2 9.8 %collective-permute-start.3 = (bf16[128,896]{1,0:T(8,128)(2,1)S(1)}, bf16[128,896]{1,0:T(8,128)(2,1)S(1)}, u32[]{:S(2)}, u32[]{:S(2)}) collective-permute-start(bf16[128,896]{1,0:T(8,128)(2,1)S(1)} %reshape.278.refs_0_), channel_id=1, source_target_pairs={{0,32},{32,0},{1,33},{33,1},{2,34},{34,2},{3,35},{35,3},{4,36},{36... | collective-permute-start | bytes 688136 | tf_op jit(solution)/shard_map/ppermute | solution.py:32
  61.0 19.4 %collective-permute-start.11 = (bf16[8,64,640]{2,1,0:T(8,128)(2,1)S(1)}, bf16[8,64,640]{2,1,0:T(8,128)(2,1)}, u32[]{:S(2)}, u32[]{:S(2)}) collective-permute-start(bf16[8,64,640]{2,1,0:T(8,128)(2,1)S(1)} %all-to-all-done.2.refs_0_), channel_id=1, source_target_pairs={{0,32},{32,0},{1,33},{33,1},{2,34},{34,2},{3,35},{35,3},{4,36},{36... | collective-permute-start | bytes 1966088 | tf_op jit(solution)/shard_map/ppermute | solution.py:32
  65.2 8.5 %collective-permute-start.10 = (bf16[128,896]{1,0:T(8,128)(2,1)S(1)}, bf16[128,896]{1,0:T(8,128)(2,1)S(1)}, u32[]{:S(2)}, u32[]{:S(2)}) collective-permute-start(bf16[128,896]{1,0:T(8,128)(2,1)S(1)} %get-tuple-element.52), channel_id=1, source_target_pairs={{0,192},{64,0},{128,64},{192,128},{1,193},{65,1},{129,65},{193,129... | collective-permute-start | bytes 688136 | tf_op jit(solution)/shard_map/ppermute | solution.py:32
  65.9 13.5 %collective-permute-start.8 = (bf16[128,896]{1,0:T(8,128)(2,1)S(1)}, bf16[128,896]{1,0:T(8,128)(2,1)S(1)}, u32[]{:S(2)}, u32[]{:S(2)}) collective-permute-start(bf16[128,896]{1,0:T(8,128)(2,1)S(1)} %get-tuple-element.54), channel_id=1, source_target_pairs={{0,64},{64,128},{128,192},{192,0},{1,65},{65,129},{129,193},{193,1... | collective-permute-start | bytes 688136 | tf_op jit(solution)/shard_map/ppermute | solution.py:32
  67.3 12.1 %collective-permute-start.9 = (bf16[128,896]{1,0:T(8,128)(2,1)S(1)}, bf16[128,896]{1,0:T(8,128)(2,1)S(1)}, u32[]{:S(2)}, u32[]{:S(2)}) collective-permute-start(bf16[128,896]{1,0:T(8,128)(2,1)S(1)} %get-tuple-element.53), channel_id=1, source_target_pairs={{0,128},{64,192},{128,0},{192,64},{1,129},{65,193},{129,1},{193,65... | collective-permute-start | bytes 688136 | tf_op jit(solution)/shard_map/ppermute | solution.py:32
  85.2 18.4 %all-to-all-start.1 = ((bf16[32,16,224]{2,1,0:T(8,128)(2,1)}), bf16[32,16,224]{2,1,0:T(8,128)(2,1)S(1)}, u32[]{:S(2)}, u32[]{:S(2)}) async-start(bf16[32,16,224]{2,1,0:T(8,128)(2,1)} %bitcast.22), calls=%async_computation.1 | async-start | bytes 524288 | tf_op jit(solution)/shard_map/all_to_all | solution.py:301
  105.7 10.7 %collective-permute-start.12 = (bf16[512,224]{1,0:T(8,128)(2,1)S(1)}, bf16[512,224]{1,0:T(8,128)(2,1)S(1)}, u32[]{:S(2)}, u32[]{:S(2)}) collective-permute-start(bf16[512,224]{1,0:T(8,128)(2,1)S(1)} %convolution_convert_fusion.refs_0_), channel_id=1, source_target_pairs={{0,192},{64,0},{128,64},{192,128},{1,193},{65,1},{129,65},{193,129... | collective-permute-start | bytes 688136 | tf_op jit(solution)/shard_map/ppermute | solution.py:32
  107.2 10.2 %collective-permute-start.13 = (bf16[512,224]{1,0:T(8,128)(2,1)S(1)}, bf16[512,224]{1,0:T(8,128)(2,1)S(1)}, u32[]{:S(2)}, u32[]{:S(2)}) collective-permute-start(bf16[512,224]{1,0:T(8,128)(2,1)S(1)} %convolution_convert_fusion.refs_0_), channel_id=1, source_target_pairs={{0,128},{64,192},{128,0},{192,64},{1,129},{65,193},{129,1},{193,65... | collective-permute-start | bytes 688136 | tf_op jit(solution)/shard_map/ppermute | solution.py:32
  107.5 12.3 %collective-permute-start.14 = (bf16[512,224]{1,0:T(8,128)(2,1)S(1)}, bf16[512,224]{1,0:T(8,128)(2,1)S(1)}, u32[]{:S(2)}, u32[]{:S(2)}) collective-permute-start(bf16[512,224]{1,0:T(8,128)(2,1)S(1)} %convolution_convert_fusion.refs_0_), channel_id=1, source_target_pairs={{0,64},{64,128},{128,192},{192,0},{1,65},{65,129},{129,193},{193,1... | collective-permute-start | bytes 688136 | tf_op jit(solution)/shard_map/ppermute | solution.py:32
  108.9 12.7 %collective-permute-start.15 = (bf16[512,224]{1,0:T(8,128)(2,1)S(1)}, bf16[512,224]{1,0:T(8,128)(2,1)S(1)}, u32[]{:S(2)}, u32[]{:S(2)}) collective-permute-start(bf16[512,224]{1,0:T(8,128)(2,1)S(1)} %convolution_convert_fusion.refs_0_), channel_id=1, source_target_pairs={{0,32},{32,0},{1,33},{33,1},{2,34},{34,2},{3,35},{35,3},{4,36},{36... | collective-permute-start | bytes 688136 | tf_op jit(solution)/shard_map/ppermute | solution.py:32
  124.7 11.3 %collective-permute-start.19 = (bf16[128,640]{1,0:T(8,128)(2,1)S(1)}, bf16[128,640]{1,0:T(8,128)(2,1)S(1)}, u32[]{:S(2)}, u32[]{:S(2)}) collective-permute-start(bf16[128,640]{1,0:T(8,128)(2,1)S(1)} %get-tuple-element.43), channel_id=1, source_target_pairs={{0,1},{1,2},{2,3},{3,0},{4,5},{5,6},{6,7},{7,4},{8,9},{9,10},{10,1... | collective-permute-start | bytes 491528 | tf_op jit(solution)/shard_map/ppermute | solution.py:32
  125.0 11.0 %collective-permute-start.20 = (bf16[128,640]{1,0:T(8,128)(2,1)S(1)}, bf16[128,640]{1,0:T(8,128)(2,1)S(1)}, u32[]{:S(2)}, u32[]{:S(2)}) collective-permute-start(bf16[128,640]{1,0:T(8,128)(2,1)S(1)} %get-tuple-element.44), channel_id=1, source_target_pairs={{0,2},{1,3},{2,0},{3,1},{4,6},{5,7},{6,4},{7,5},{8,10},{9,11},{10,... | collective-permute-start | bytes 491528 | tf_op jit(solution)/shard_map/ppermute | solution.py:32
  127.5 9.2 %collective-permute-start.21 = (bf16[128,640]{1,0:T(8,128)(2,1)S(1)}, bf16[128,640]{1,0:T(8,128)(2,1)}, u32[]{:S(2)}, u32[]{:S(2)}) collective-permute-start(bf16[128,640]{1,0:T(8,128)(2,1)S(1)} %get-tuple-element.45), channel_id=1, source_target_pairs={{0,3},{1,0},{2,1},{3,2},{4,7},{5,4},{6,5},{7,6},{8,11},{9,8},{10,9... | collective-permute-start | bytes 491528 | tf_op jit(solution)/shard_map/ppermute | solution.py:32
  138.7 6.7 %collective-permute-start.22 = (bf16[128,640]{1,0:T(8,128)(2,1)S(1)}, bf16[128,640]{1,0:T(8,128)(2,1)S(1)}, u32[]{:S(2)}, u32[]{:S(2)}) collective-permute-start(bf16[128,640]{1,0:T(8,128)(2,1)S(1)} %get-tuple-element.56.refs_0_), channel_id=1, source_target_pairs={{0,28},{4,0},{8,4},{12,8},{16,12},{20,16},{24,20},{28,24},{1,29},{... | collective-permute-start | bytes 491528 | tf_op jit(solution)/shard_map/ppermute | solution.py:32
  166.9 7.6 %collective-permute-start.29 = (bf16[160,640]{1,0:T(8,128)(2,1)S(1)}, bf16[160,640]{1,0:T(8,128)(2,1)S(1)}, u32[]{:S(2)}, u32[]{:S(2)}) collective-permute-start(bf16[160,640]{1,0:T(8,128)(2,1)S(1)} %get-tuple-element.49), channel_id=1, source_target_pairs={{0,1},{1,2},{2,3},{3,0},{4,5},{5,6},{6,7},{7,4},{8,9},{9,10},{10,1... | collective-permute-start | bytes 614408 | tf_op jit(solution)/shard_map/ppermute | solution.py:32
  168.8 8.9 %collective-permute-start.30 = (bf16[160,640]{1,0:T(8,128)(2,1)S(1)}, bf16[160,640]{1,0:T(8,128)(2,1)S(1)}, u32[]{:S(2)}, u32[]{:S(2)}) collective-permute-start(bf16[160,640]{1,0:T(8,128)(2,1)S(1)} %get-tuple-element.50), channel_id=1, source_target_pairs={{0,2},{1,3},{2,0},{3,1},{4,6},{5,7},{6,4},{7,5},{8,10},{9,11},{10,... | collective-permute-start | bytes 614408 | tf_op jit(solution)/shard_map/ppermute | solution.py:32
  (21 other events, 126.0 us)
Sparse Core Ops, SparseCore 0:
  10.7 29.3 all-gather.5
  41.9 41.1 all-gather.3
  85.6 39.7 reduce-scatter.1

commit v4 on v3

--- a/solution.py
+++ b/solution.py
@@ -234,11 +234,10 @@
 
     weight_rows = student_weight.shape[0]
     in_wave = (routes < owners).T
-    high = lax.reduce_precision(route_weights.T, 8, 7)
     info = jnp.concatenate(
-        [jnp.where(in_wave, routes.T, -64), jnp.where(in_wave, slots.T, 0), high, route_weights.T - high]
+        [jnp.where(in_wave, routes.T, -64), jnp.where(in_wave, slots.T, 0), route_weights.T]
     ).astype(BF)
-    info = jnp.pad(info, ((0, 16), (0, student_weight.shape[1] - tokens)))
+    info = jnp.pad(info, ((0, 24), (0, student_weight.shape[1] - tokens)))
     weight_info = jnp.concatenate([student_weight, info])
     gathered = lax.all_gather(weight_info, "y", axis=0)
 
@@ -257,14 +256,14 @@
     projector_z = lax.all_gather(after(projector, weight_info), "z", axis=0, tiled=True).reshape(
         zs, projector.shape[0], projector.shape[1]
     )
-    plans = gathered[:, weight_rows : weight_rows + 32, :tokens].astype(F32)
+    plans = gathered[:, weight_rows : weight_rows + 24, :tokens].astype(F32)
     plans = lax.dynamic_slice_in_dim(jnp.concatenate([plans, plans]), y, ys, 0)
     combine_rows = []
     row_ids = jnp.arange(slot_count * ys, dtype=jnp.int32)[None, :]
     for hop in range(ys):
         plan = plans[hop]
         place = plan[:8] * (ys * CAP) + plan[8:16] + (((y + hop) % ys) * CAP).astype(F32)
-        place, share = place.astype(jnp.int32), plan[16:24] + plan[24:32]
+        place, share = place.astype(jnp.int32), plan[16:24]
         part = jnp.zeros((tokens, slot_count * ys), F32)
         for k in range(8):
             part = part + jnp.where(place[k][:, None] == row_ids, share[k][:, None], 0.0)

time: 186 us -> 182 us (0.978)
  waiting for transfers between devices: 81.6 us -> 75.2 us
  local copies, waits for them, and re-layouts: 6.58 us -> 11.4 us
  starting transfers between devices: 55.1 us -> 53.2 us
    ppermute x32, waiting for transfers between devices: 65.2 us -> 58.8 us  [shifted(): lax.ppermute(value, axis, [(i, (i - hop) % size) for i in range(size)])]
    unnamed x14 -> x26, local copies, waits for them, and re-layouts: 2.38 us -> 7.27 us
    all_to_all x1, starting transfers between devices: 8.65 us -> 6.65 us  [body(): lax.all_to_all(outgoing_rows.reshape(owners, ys * CAP, width // ys), fsdp...]
where the time goes in v4:
time: 182 us
  waiting for transfers between devices  75.2 us (41%)
  starting transfers between devices  53.2 us (29%)
  Pallas kernels  15.9 us (9%)
  between operations  14.1 us (8%)
  local copies, waits for them, and re-layouts  11.4 us (6%)
  other arithmetic  10.2 us (6%)
    ppermute x32, waiting for transfers between devices, shifted(): lax.ppermute(value, axis, [(i, (i - hop) % size) for i in range(size)])  58.8 us
    ppermute x32, starting transfers between devices, shifted(): lax.ppermute(value, axis, [(i, (i - hop) % size) for i in range(size)])  30.2 us
    all_to_all x1, starting transfers between devices, body(): lax.all_to_all(outgoing.reshape(owners, CAP, width), fsdp, split_axis=0,...  10.5 us
    all_to_all x1, waiting for transfers between devices, body(): lax.all_to_all(outgoing.reshape(owners, CAP, width), fsdp, split_axis=0,...  8.74 us
    unnamed x26, local copies, waits for them, and re-layouts  7.27 us
    all_to_all x1, waiting for transfers between devices, body(): lax.all_to_all(outgoing_rows.reshape(owners, ys * CAP, width // ys), fsdp...  6.95 us
    all_to_all x1, starting transfers between devices, body(): lax.all_to_all(outgoing_rows.reshape(owners, ys * CAP, width // ys), fsdp...  6.65 us
    all_to_all x1, starting transfers between devices, body(): half = lax.all_to_all(half, 'z', split_axis=0, concat_axis=0, tiled=True)  5.9 us
  transfers between devices with their start and end apart: 38, of which 20 were waited for; matrix products, arithmetic and copies ran while one was open for 5% of the time, Pallas kernels for 8%

profile of v4, /device:TPU:96, one launch (start us, length us, event | category | flops | bytes accessed | tf_op | source)
XLA Modules:
  0.0 181.7 jit_solution(18433971642822929481)
XLA Ops:
  12.3 10.5 %all-to-all-start = ((bf16[32,4,896]{2,1,0:T(4,128)(2,1)}), bf16[32,4,896]{2,1,0:T(4,128)(2,1)S(1)}, u32[]{:S(2)}, u32[]{:S(2)}) async-start(bf16[32,4,896]{2,1,0:T(4,128)(2,1)} %reshape.269), calls=%async_computation | async-start | bytes 458752 | tf_op jit(solution)/shard_map/all_to_all | solution.py:252
  24.0 8.7 %all-to-all-done = bf16[32,4,896]{2,1,0:T(4,128)(2,1)S(1)} async-done(((bf16[32,4,896]{2,1,0:T(4,128)(2,1)}), bf16[32,4,896]{2,1,0:T(4,128)(2,1)S(1)}, u32[]{:S(2)}, u32[]{:S(2)}) %all-to-all-start) | async-done | bytes 229408 | tf_op jit(solution)/shard_map/all_to_all | solution.py:252
  32.9 2.8 %collective-permute-start = (bf16[128,896]{1,0:T(8,128)(2,1)S(1)}, bf16[128,896]{1,0:T(8,128)(2,1)S(1)}, u32[]{:S(2)}, u32[]{:S(2)}) collective-permute-start(bf16[128,896]{1,0:T(8,128)(2,1)S(1)} %reshape.270.refs_0_), channel_id=1, source_target_pairs={{0,192},{64,0},{128,64},{192,128},{1,193},{65,1},{129,65},{193,129... | collective-permute-start | bytes 688136 | tf_op jit(solution)/shard_map/ppermute | solution.py:32
  37.4 5.9 %all-to-all-start.2 = ((bf16[8,64,640]{2,1,0:T(8,128)(2,1)}), bf16[8,64,640]{2,1,0:T(8,128)(2,1)S(1)}, u32[]{:S(2)}, u32[]{:S(2)}) async-start(bf16[8,64,640]{2,1,0:T(8,128)(2,1)} %bitcast.183), calls=%async_computation.2 | async-start | bytes 1310720 | tf_op jit(solution)/shard_map/all_to_all | solution.py:285
  53.0 5.3 %expert_ffn.1 = (bf16[4,128,896]{2,1,0:T(8,128)(2,1)S(1)}, bf16[4,128,896]{2,1,0:T(8,128)(2,1)}) custom-call(s32[8]{0:T(128)S(1)} %pad_add_fusion.order, bf16[128,896]{1,0:T(8,128)(2,1)S(1)} %copy-done.3, bf16[128,896]{1,0:T(8,128)(2,1)S(1)} %copy-done.6, bf16[128,896]{1,0:T(8,128)(2,1)S(1)} %copy-done.8, bf16[128,896]{1,0:T(8,128)(2,1)S(1)} %copy-done.10, ...), custom_call_target="tpu_custom_call" | custom-call | tf_op jit(solution)/shard_map/expert_ffn/pallas_call | solution.py:80
  66.5 8.5 %collective-permute-done.10.d = bf16[128,896]{1,0:T(8,128)(2,1)S(1)} collective-permute-done((bf16[128,896]{1,0:T(8,128)(2,1)S(1)}, bf16[128,896]{1,0:T(8,128)(2,1)S(1)}, u32[]{:S(2)}, u32[]{:S(2)}) %collective-permute-start.10) | collective-permute-done | bytes 229408 | tf_op jit(solution)/shard_map/ppermute | solution.py:32
  75.0 3.4 %collective-permute-done.8.b = bf16[128,896]{1,0:T(8,128)(2,1)S(1)} collective-permute-done((bf16[128,896]{1,0:T(8,128)(2,1)S(1)}, bf16[128,896]{1,0:T(8,128)(2,1)S(1)}, u32[]{:S(2)}, u32[]{:S(2)}) %collective-permute-start.8) | collective-permute-done | bytes 229408 | tf_op jit(solution)/shard_map/ppermute | solution.py:32
  79.2 3.7 %student.1 = (bf16[1024,640]{1,0:T(8,128)(2,1)}, bf16[8,128,640]{2,1,0:T(8,128)(2,1)}) custom-call(s32[2]{0:T(128)S(1)} %pad_add_fusion.2.order, bf16[8,64,640]{2,1,0:T(8,128)(2,1)S(1)} %all-to-all-done.2.refs_0_, bf16[8,64,640]{2,1,0:T(8,128)(2,1)} %collective-permute-done.11.refs_1_, bf16[4,208,640]{2,1,0:T(8,128)(2,1)S(1)} %bitcast.182), custom_call_target="tpu_custom_call" | custom-call | tf_op jit(solution)/shard_map/student/pallas_call | solution.py:201
  83.8 6.6 %all-to-all-start.1 = ((bf16[32,16,224]{2,1,0:T(8,128)(2,1)}), bf16[32,16,224]{2,1,0:T(8,128)(2,1)S(1)}, u32[]{:S(2)}, u32[]{:S(2)}) async-start(bf16[32,16,224]{2,1,0:T(8,128)(2,1)} %bitcast.22), calls=%async_computation.1 | async-start | bytes 524288 | tf_op jit(solution)/shard_map/all_to_all | solution.py:300
  93.6 7.0 %all-to-all-done.1 = bf16[32,16,224]{2,1,0:T(8,128)(2,1)S(1)} async-done(((bf16[32,16,224]{2,1,0:T(8,128)(2,1)}), bf16[32,16,224]{2,1,0:T(8,128)(2,1)S(1)}, u32[]{:S(2)}, u32[]{:S(2)}) %all-to-all-start.1) | async-done | bytes 229408 | tf_op jit(solution)/shard_map/all_to_all | solution.py:300
  104.9 6.7 %collective-permute-done.12.refs_1_ = bf16[512,224]{1,0:T(8,128)(2,1)S(1)} collective-permute-done((bf16[512,224]{1,0:T(8,128)(2,1)S(1)}, bf16[512,224]{1,0:T(8,128)(2,1)S(1)}, u32[]{:S(2)}, u32[]{:S(2)}) %collective-permute-start.12) | collective-permute-done | bytes 229408 | tf_op jit(solution)/shard_map/ppermute | solution.py:32
  113.8 2.7 %collective-permute-done.14.refs_3_ = bf16[512,224]{1,0:T(8,128)(2,1)S(1)} collective-permute-done((bf16[512,224]{1,0:T(8,128)(2,1)S(1)}, bf16[512,224]{1,0:T(8,128)(2,1)S(1)}, u32[]{:S(2)}, u32[]{:S(2)}) %collective-permute-start.14) | collective-permute-done | bytes 229408 | tf_op jit(solution)/shard_map/ppermute | solution.py:32
  118.3 2.4 %project.1 = (f32[128,640]{1,0:T(8,128)S(1)}, bf16[128,640]{1,0:T(8,128)(2,1)S(1)}, bf16[128,640]{1,0:T(8,128)(2,1)S(1)}, bf16[128,640]{1,0:T(8,128)(2,1)S(1)}) custom-call(s32[8]{0:T(128)S(1)} %pad_add_fusion.order, bf16[512,224]{1,0:T(8,128)(2,1)S(1)} %convolution_convert_fusion.refs_0_, bf16[512,224]{1,0:T(8,128)(2,1)S(1)} %collective-permute-done.12.refs_1_, ...), custom_call_target="tpu_custom_call" | custom-call | tf_op jit(solution)/shard_map/project/pallas_call | solution.py:142
  121.7 2.5 %collective-permute-start.20 = (bf16[128,640]{1,0:T(8,128)(2,1)S(1)}, bf16[128,640]{1,0:T(8,128)(2,1)S(1)}, u32[]{:S(2)}, u32[]{:S(2)}) collective-permute-start(bf16[128,640]{1,0:T(8,128)(2,1)S(1)} %get-tuple-element.44), channel_id=1, source_target_pairs={{0,2},{1,3},{2,0},{3,1},{4,6},{5,7},{6,4},{7,5},{8,10},{9,11},{10,... | collective-permute-start | bytes 491528 | tf_op jit(solution)/shard_map/ppermute | solution.py:32
  125.9 6.7 %collective-permute-done.19 = bf16[128,640]{1,0:T(8,128)(2,1)S(1)} collective-permute-done((bf16[128,640]{1,0:T(8,128)(2,1)S(1)}, bf16[128,640]{1,0:T(8,128)(2,1)S(1)}, u32[]{:S(2)}, u32[]{:S(2)}) %collective-permute-start.19) | collective-permute-done | bytes 163872 | tf_op jit(solution)/shard_map/ppermute | solution.py:32
  138.6 3.5 %collective-permute-done.22.refs_1_ = bf16[128,640]{1,0:T(8,128)(2,1)S(1)} collective-permute-done((bf16[128,640]{1,0:T(8,128)(2,1)S(1)}, bf16[128,640]{1,0:T(8,128)(2,1)S(1)}, u32[]{:S(2)}, u32[]{:S(2)}) %collective-permute-start.22) | collective-permute-done | bytes 163872 | tf_op jit(solution)/shard_map/ppermute | solution.py:32
  142.3 2.9 %collective-permute-start.27 = (bf16[128,640]{1,0:T(8,128)(2,1)S(1)}, bf16[128,640]{1,0:T(8,128)(2,1)S(1)}, u32[]{:S(2)}, u32[]{:S(2)}) collective-permute-start(bf16[128,640]{1,0:T(8,128)(2,1)S(1)} %collective-permute-done.26.refs_5_), channel_id=1, source_target_pairs={{0,4},{4,8},{8,12},{12,16},{16,20},{20,24},{24,28},{28,0},{1,5},{5... | collective-permute-start | bytes 491528 | tf_op jit(solution)/shard_map/ppermute | solution.py:32
  145.3 3.3 %collective-permute-done.23.refs_2_ = bf16[128,640]{1,0:T(8,128)(2,1)S(1)} collective-permute-done((bf16[128,640]{1,0:T(8,128)(2,1)S(1)}, bf16[128,640]{1,0:T(8,128)(2,1)S(1)}, u32[]{:S(2)}, u32[]{:S(2)}) %collective-permute-start.23) | collective-permute-done | bytes 163872 | tf_op jit(solution)/shard_map/ppermute | solution.py:32
  148.6 3.2 %collective-permute-start.28 = (bf16[128,640]{1,0:T(8,128)(2,1)S(1)}, bf16[128,640]{1,0:T(8,128)(2,1)S(1)}, u32[]{:S(2)}, u32[]{:S(2)}) collective-permute-start(bf16[128,640]{1,0:T(8,128)(2,1)S(1)} %collective-permute-done.27.refs_6_), channel_id=1, source_target_pairs={{0,4},{4,8},{8,12},{12,16},{16,20},{20,24},{24,28},{28,0},{1,5},{5... | collective-permute-start | bytes 491528 | tf_op jit(solution)/shard_map/ppermute | solution.py:32
  151.8 3.3 %collective-permute-done.24.refs_3_ = bf16[128,640]{1,0:T(8,128)(2,1)S(1)} collective-permute-done((bf16[128,640]{1,0:T(8,128)(2,1)S(1)}, bf16[128,640]{1,0:T(8,128)(2,1)S(1)}, u32[]{:S(2)}, u32[]{:S(2)}) %collective-permute-start.24) | collective-permute-done | bytes 163872 | tf_op jit(solution)/shard_map/ppermute | solution.py:32
  155.1 6.5 %collective-permute-done.25.refs_4_ = bf16[128,640]{1,0:T(8,128)(2,1)S(1)} collective-permute-done((bf16[128,640]{1,0:T(8,128)(2,1)S(1)}, bf16[128,640]{1,0:T(8,128)(2,1)S(1)}, u32[]{:S(2)}, u32[]{:S(2)}) %collective-permute-start.25) | collective-permute-done | bytes 163872 | tf_op jit(solution)/shard_map/ppermute | solution.py:32
  165.4 2.9 %collective-permute-start.30 = (bf16[160,640]{1,0:T(8,128)(2,1)S(1)}, bf16[160,640]{1,0:T(8,128)(2,1)S(1)}, u32[]{:S(2)}, u32[]{:S(2)}) collective-permute-start(bf16[160,640]{1,0:T(8,128)(2,1)S(1)} %get-tuple-element.50), channel_id=1, source_target_pairs={{0,2},{1,3},{2,0},{3,1},{4,6},{5,7},{6,4},{7,5},{8,10},{9,11},{10,... | collective-permute-start | bytes 614408 | tf_op jit(solution)/shard_map/ppermute | solution.py:32
  168.4 2.9 %collective-permute-done.29 = bf16[160,640]{1,0:T(8,128)(2,1)S(1)} collective-permute-done((bf16[160,640]{1,0:T(8,128)(2,1)S(1)}, bf16[160,640]{1,0:T(8,128)(2,1)S(1)}, u32[]{:S(2)}, u32[]{:S(2)}) %collective-permute-start.29) | collective-permute-done | bytes 204832 | tf_op jit(solution)/shard_map/ppermute | solution.py:32
  171.2 3.0 %collective-permute-done.30 = bf16[160,640]{1,0:T(8,128)(2,1)S(1)} collective-permute-done((bf16[160,640]{1,0:T(8,128)(2,1)S(1)}, bf16[160,640]{1,0:T(8,128)(2,1)S(1)}, u32[]{:S(2)}, u32[]{:S(2)}) %collective-permute-start.30) | collective-permute-done | bytes 204832 | tf_op jit(solution)/shard_map/ppermute | solution.py:32
  (120 shorter events, 52.6 us)
Async XLA Ops:
  7.2 51.7 %all-gather.6.cloned.1.call-start = ((), (), s32[]{:S(2)}) async-start(), calls=%async_computation.6 | async-start | bytes 1331200 | tf_op jit(solution)/shard_map/all_gather | solution.py:242
  10.5 92.1 %all-gather.4.cloned.1.call-start = ((), (), s32[]{:S(2)}) async-start(), calls=%async_computation.4 | async-start | bytes 2580480 | tf_op jit(solution)/shard_map/all_gather | solution.py:256
  12.3 20.5 %all-to-all-start = ((bf16[32,4,896]{2,1,0:T(4,128)(2,1)}), bf16[32,4,896]{2,1,0:T(4,128)(2,1)S(1)}, u32[]{:S(2)}, u32[]{:S(2)}) async-start(bf16[32,4,896]{2,1,0:T(4,128)(2,1)} %reshape.269), calls=%async_computation | async-start | bytes 458752 | tf_op jit(solution)/shard_map/all_to_all | solution.py:252
  32.9 11.1 %collective-permute-start = (bf16[128,896]{1,0:T(8,128)(2,1)S(1)}, bf16[128,896]{1,0:T(8,128)(2,1)S(1)}, u32[]{:S(2)}, u32[]{:S(2)}) collective-permute-start(bf16[128,896]{1,0:T(8,128)(2,1)S(1)} %reshape.270.refs_0_), channel_id=1, source_target_pairs={{0,192},{64,0},{128,64},{192,128},{1,193},{65,1},{129,65},{193,129... | collective-permute-start | bytes 688136 | tf_op jit(solution)/shard_map/ppermute | solution.py:32
  35.7 9.7 %collective-permute-start.1 = (bf16[128,896]{1,0:T(8,128)(2,1)S(1)}, bf16[128,896]{1,0:T(8,128)(2,1)S(1)}, u32[]{:S(2)}, u32[]{:S(2)}) collective-permute-start(bf16[128,896]{1,0:T(8,128)(2,1)S(1)} %reshape.270.refs_0_), channel_id=1, source_target_pairs={{0,128},{64,192},{128,0},{192,64},{1,129},{65,193},{129,1},{193,65... | collective-permute-start | bytes 688136 | tf_op jit(solution)/shard_map/ppermute | solution.py:32
  36.5 11.2 %collective-permute-start.2 = (bf16[128,896]{1,0:T(8,128)(2,1)S(1)}, bf16[128,896]{1,0:T(8,128)(2,1)S(1)}, u32[]{:S(2)}, u32[]{:S(2)}) collective-permute-start(bf16[128,896]{1,0:T(8,128)(2,1)S(1)} %reshape.270.refs_0_), channel_id=1, source_target_pairs={{0,64},{64,128},{128,192},{192,0},{1,65},{65,129},{129,193},{193,1... | collective-permute-start | bytes 688136 | tf_op jit(solution)/shard_map/ppermute | solution.py:32
  37.4 21.1 %all-to-all-start.2 = ((bf16[8,64,640]{2,1,0:T(8,128)(2,1)}), bf16[8,64,640]{2,1,0:T(8,128)(2,1)S(1)}, u32[]{:S(2)}, u32[]{:S(2)}) async-start(bf16[8,64,640]{2,1,0:T(8,128)(2,1)} %bitcast.183), calls=%async_computation.2 | async-start | bytes 1310720 | tf_op jit(solution)/shard_map/all_to_all | solution.py:285
  43.3 90.1 %reduce-scatter.2.cloned.1.call-start = ((), (), s32[]{:S(2)}) async-start(), calls=%async_computation.5 | async-start | bytes 1474560 | tf_op jit(solution)/shard_map/reduce_scatter | solution.py:299
  58.5 20.7 %collective-permute-start.11 = (bf16[8,64,640]{2,1,0:T(8,128)(2,1)S(1)}, bf16[8,64,640]{2,1,0:T(8,128)(2,1)}, u32[]{:S(2)}, u32[]{:S(2)}) collective-permute-start(bf16[8,64,640]{2,1,0:T(8,128)(2,1)S(1)} %all-to-all-done.2.refs_0_), channel_id=1, source_target_pairs={{0,32},{32,0},{1,33},{33,1},{2,34},{34,2},{3,35},{35,3},{4,36},{36... | collective-permute-start | bytes 1966088 | tf_op jit(solution)/shard_map/ppermute | solution.py:32
  62.8 12.2 %collective-permute-start.10 = (bf16[128,896]{1,0:T(8,128)(2,1)S(1)}, bf16[128,896]{1,0:T(8,128)(2,1)S(1)}, u32[]{:S(2)}, u32[]{:S(2)}) collective-permute-start(bf16[128,896]{1,0:T(8,128)(2,1)S(1)} %get-tuple-element.52), channel_id=1, source_target_pairs={{0,192},{64,0},{128,64},{192,128},{1,193},{65,1},{129,65},{193,129... | collective-permute-start | bytes 688136 | tf_op jit(solution)/shard_map/ppermute | solution.py:32
  64.8 13.5 %collective-permute-start.8 = (bf16[128,896]{1,0:T(8,128)(2,1)S(1)}, bf16[128,896]{1,0:T(8,128)(2,1)S(1)}, u32[]{:S(2)}, u32[]{:S(2)}) collective-permute-start(bf16[128,896]{1,0:T(8,128)(2,1)S(1)} %get-tuple-element.54), channel_id=1, source_target_pairs={{0,64},{64,128},{128,192},{192,0},{1,65},{65,129},{129,193},{193,1... | collective-permute-start | bytes 688136 | tf_op jit(solution)/shard_map/ppermute | solution.py:32
  64.9 13.5 %collective-permute-start.9 = (bf16[128,896]{1,0:T(8,128)(2,1)S(1)}, bf16[128,896]{1,0:T(8,128)(2,1)S(1)}, u32[]{:S(2)}, u32[]{:S(2)}) collective-permute-start(bf16[128,896]{1,0:T(8,128)(2,1)S(1)} %get-tuple-element.53), channel_id=1, source_target_pairs={{0,128},{64,192},{128,0},{192,64},{1,129},{65,193},{129,1},{193,65... | collective-permute-start | bytes 688136 | tf_op jit(solution)/shard_map/ppermute | solution.py:32
  83.8 16.8 %all-to-all-start.1 = ((bf16[32,16,224]{2,1,0:T(8,128)(2,1)}), bf16[32,16,224]{2,1,0:T(8,128)(2,1)S(1)}, u32[]{:S(2)}, u32[]{:S(2)}) async-start(bf16[32,16,224]{2,1,0:T(8,128)(2,1)} %bitcast.22), calls=%async_computation.1 | async-start | bytes 524288 | tf_op jit(solution)/shard_map/all_to_all | solution.py:300
  102.7 9.0 %collective-permute-start.12 = (bf16[512,224]{1,0:T(8,128)(2,1)S(1)}, bf16[512,224]{1,0:T(8,128)(2,1)S(1)}, u32[]{:S(2)}, u32[]{:S(2)}) collective-permute-start(bf16[512,224]{1,0:T(8,128)(2,1)S(1)} %convolution_convert_fusion.refs_0_), channel_id=1, source_target_pairs={{0,192},{64,0},{128,64},{192,128},{1,193},{65,1},{129,65},{193,129... | collective-permute-start | bytes 688136 | tf_op jit(solution)/shard_map/ppermute | solution.py:32
  103.3 10.5 %collective-permute-start.13 = (bf16[512,224]{1,0:T(8,128)(2,1)S(1)}, bf16[512,224]{1,0:T(8,128)(2,1)S(1)}, u32[]{:S(2)}, u32[]{:S(2)}) collective-permute-start(bf16[512,224]{1,0:T(8,128)(2,1)S(1)} %convolution_convert_fusion.refs_0_), channel_id=1, source_target_pairs={{0,128},{64,192},{128,0},{192,64},{1,129},{65,193},{129,1},{193,65... | collective-permute-start | bytes 688136 | tf_op jit(solution)/shard_map/ppermute | solution.py:32
  103.8 12.7 %collective-permute-start.14 = (bf16[512,224]{1,0:T(8,128)(2,1)S(1)}, bf16[512,224]{1,0:T(8,128)(2,1)S(1)}, u32[]{:S(2)}, u32[]{:S(2)}) collective-permute-start(bf16[512,224]{1,0:T(8,128)(2,1)S(1)} %convolution_convert_fusion.refs_0_), channel_id=1, source_target_pairs={{0,64},{64,128},{128,192},{192,0},{1,65},{65,129},{129,193},{193,1... | collective-permute-start | bytes 688136 | tf_op jit(solution)/shard_map/ppermute | solution.py:32
  104.9 13.3 %collective-permute-start.15 = (bf16[512,224]{1,0:T(8,128)(2,1)S(1)}, bf16[512,224]{1,0:T(8,128)(2,1)S(1)}, u32[]{:S(2)}, u32[]{:S(2)}) collective-permute-start(bf16[512,224]{1,0:T(8,128)(2,1)S(1)} %convolution_convert_fusion.refs_0_), channel_id=1, source_target_pairs={{0,32},{32,0},{1,33},{33,1},{2,34},{34,2},{3,35},{35,3},{4,36},{36... | collective-permute-start | bytes 688136 | tf_op jit(solution)/shard_map/ppermute | solution.py:32
  111.6 6.6 %collective-permute-start.16 = (bf16[512,224]{1,0:T(8,128)(2,1)S(1)}, bf16[512,224]{1,0:T(8,128)(2,1)S(1)}, u32[]{:S(2)}, u32[]{:S(2)}) collective-permute-start(bf16[512,224]{1,0:T(8,128)(2,1)S(1)} %collective-permute-done.12.refs_1_), channel_id=1, source_target_pairs={{0,32},{32,0},{1,33},{33,1},{2,34},{34,2},{3,35},{35,3},{4,36},{36... | collective-permute-start | bytes 688136 | tf_op jit(solution)/shard_map/ppermute | solution.py:32
  121.4 11.3 %collective-permute-start.19 = (bf16[128,640]{1,0:T(8,128)(2,1)S(1)}, bf16[128,640]{1,0:T(8,128)(2,1)S(1)}, u32[]{:S(2)}, u32[]{:S(2)}) collective-permute-start(bf16[128,640]{1,0:T(8,128)(2,1)S(1)} %get-tuple-element.43), channel_id=1, source_target_pairs={{0,1},{1,2},{2,3},{3,0},{4,5},{5,6},{6,7},{7,4},{8,9},{9,10},{10,1... | collective-permute-start | bytes 491528 | tf_op jit(solution)/shard_map/ppermute | solution.py:32
  121.7 10.9 %collective-permute-start.20 = (bf16[128,640]{1,0:T(8,128)(2,1)S(1)}, bf16[128,640]{1,0:T(8,128)(2,1)S(1)}, u32[]{:S(2)}, u32[]{:S(2)}) collective-permute-start(bf16[128,640]{1,0:T(8,128)(2,1)S(1)} %get-tuple-element.44), channel_id=1, source_target_pairs={{0,2},{1,3},{2,0},{3,1},{4,6},{5,7},{6,4},{7,5},{8,10},{9,11},{10,... | collective-permute-start | bytes 491528 | tf_op jit(solution)/shard_map/ppermute | solution.py:32
  124.3 9.1 %collective-permute-start.21 = (bf16[128,640]{1,0:T(8,128)(2,1)S(1)}, bf16[128,640]{1,0:T(8,128)(2,1)}, u32[]{:S(2)}, u32[]{:S(2)}) collective-permute-start(bf16[128,640]{1,0:T(8,128)(2,1)S(1)} %get-tuple-element.45), channel_id=1, source_target_pairs={{0,3},{1,0},{2,1},{3,2},{4,7},{5,4},{6,5},{7,6},{8,11},{9,8},{10,9... | collective-permute-start | bytes 491528 | tf_op jit(solution)/shard_map/ppermute | solution.py:32
  135.3 6.7 %collective-permute-start.22 = (bf16[128,640]{1,0:T(8,128)(2,1)S(1)}, bf16[128,640]{1,0:T(8,128)(2,1)S(1)}, u32[]{:S(2)}, u32[]{:S(2)}) collective-permute-start(bf16[128,640]{1,0:T(8,128)(2,1)S(1)} %get-tuple-element.56.refs_0_), channel_id=1, source_target_pairs={{0,28},{4,0},{8,4},{12,8},{16,12},{20,16},{24,20},{28,24},{1,29},{... | collective-permute-start | bytes 491528 | tf_op jit(solution)/shard_map/ppermute | solution.py:32
  163.5 7.7 %collective-permute-start.29 = (bf16[160,640]{1,0:T(8,128)(2,1)S(1)}, bf16[160,640]{1,0:T(8,128)(2,1)S(1)}, u32[]{:S(2)}, u32[]{:S(2)}) collective-permute-start(bf16[160,640]{1,0:T(8,128)(2,1)S(1)} %get-tuple-element.49), channel_id=1, source_target_pairs={{0,1},{1,2},{2,3},{3,0},{4,5},{5,6},{6,7},{7,4},{8,9},{9,10},{10,1... | collective-permute-start | bytes 614408 | tf_op jit(solution)/shard_map/ppermute | solution.py:32
  165.4 8.8 %collective-permute-start.30 = (bf16[160,640]{1,0:T(8,128)(2,1)S(1)}, bf16[160,640]{1,0:T(8,128)(2,1)S(1)}, u32[]{:S(2)}, u32[]{:S(2)}) collective-permute-start(bf16[160,640]{1,0:T(8,128)(2,1)S(1)} %get-tuple-element.50), channel_id=1, source_target_pairs={{0,2},{1,3},{2,0},{3,1},{4,6},{5,7},{6,4},{7,5},{8,10},{9,11},{10,... | collective-permute-start | bytes 614408 | tf_op jit(solution)/shard_map/ppermute | solution.py:32
  (27 other events, 128.4 us)
Sparse Core Ops, SparseCore 0:
  10.7 29.3 all-gather.5
  41.9 42.0 all-gather.3
  86.5 37.5 reduce-scatter.1

commit v5 on v4

--- a/solution.py
+++ b/solution.py
@@ -39,8 +39,11 @@
 
 
 def ffn_kernel(order, *refs):
-    blocks, hbm, (keep, send), (both, down, sems) = refs[:8], refs[8:11], refs[11:13], refs[13:]
+    blocks, hbm, (keep, send), (both, down, near, sems) = refs[:8], refs[8:11], refs[11:13], refs[13:]
     width = blocks[0].shape[1]
+    moves = [pltpu.make_async_copy(blocks[k], near.at[k], sems.at[17 + k]) for k in range(4)]
+    for move in moves:
+        move.start()
     hidden_units = down.shape[0]
 
     def rows(k):
@@ -61,7 +64,10 @@
     for k in range(8):
         copies[2 * k].wait()
         copies[2 * k + 1].wait()
-        acts += jnp.dot(blocks[k][...], both[rows(k), :], preferred_element_type=F32)
+        if k < 4:
+            moves[k].wait()
+        block = near[k] if k < 4 else blocks[k][...]
+        acts += jnp.dot(block, both[rows(k), :], preferred_element_type=F32)
     gate_act, up_act = acts[:, :hidden_units], acts[:, hidden_units:]
     copies[16].wait()
     hidden = (gate_act / (1.0 + jnp.exp(-gate_act)) * up_act).astype(BF)
@@ -80,13 +86,16 @@
     return pl.pallas_call(
         ffn_kernel,
         out_shape=(shape, shape),
-        in_specs=[SMEM] + [VMEM] * 8 + [pl.BlockSpec(memory_space=pltpu.HBM)] * 3,
+        in_specs=[SMEM]
+        + [pl.BlockSpec(memory_space=pltpu.HBM)] * 4
+        + [VMEM] * 4
+        + [pl.BlockSpec(memory_space=pltpu.HBM)] * 3,
         out_specs=(VMEM, VMEM),
         scratch_shapes=[pltpu.VMEM((gate.shape[0], 2 * gate.shape[1]), BF), pltpu.VMEM(down.shape, BF)]
-        + [pltpu.SemaphoreType.DMA((17,))],
+        + [pltpu.VMEM((4, rows, width), BF), pltpu.SemaphoreType.DMA((21,))],
         compiler_params=limit(16),
         name="expert_ffn",
-    )(order, *blocks, in_hbm(gate), in_hbm(up), in_hbm(down))
+    )(order, *map(in_hbm, blocks[:4]), *blocks[4:], in_hbm(gate), in_hbm(up), in_hbm(down))
 
 
 def fold_kernel(a, b, c, d, out):

time: 182 us -> 183 us (level)
  local copies, waits for them, and re-layouts: 11.4 us -> 5.63 us
  waiting for transfers between devices: 75.2 us -> 79.6 us
  starting transfers between devices: 53.2 us -> 55.1 us
    unnamed x26 -> x18, local copies, waits for them, and re-layouts: 7.27 us -> 1.45 us
    all_to_all x1, waiting for transfers between devices: 0.01 us -> 2.93 us  [body(): half = lax.all_to_all(half, 'z', split_axis=0, concat_axis=0, tiled=True)]
  transfers between devices with their start and end apart: 38 -> 38, of which waited for: 20 -> 21; matrix products, arithmetic and copies ran while one was open for 5% -> 5% of each run, Pallas kernels for 8% -> 8%
where the time goes in v5:
time: 183 us; the launch traced here: 182 us
  waiting for transfers between devices  79.6 us (43%)
  starting transfers between devices  55.1 us (30%)
  Pallas kernels  16.1 us (9%)
  between operations  14.1 us (8%)
  other arithmetic  10.2 us (6%)
  local copies, waits for them, and re-layouts  5.63 us (3%)
    ppermute x32, waiting for transfers between devices, shifted(): lax.ppermute(value, axis, [(i, (i - hop) % size) for i in range(size)])  59.4 us
    ppermute x32, starting transfers between devices, shifted(): lax.ppermute(value, axis, [(i, (i - hop) % size) for i in range(size)])  30.9 us
    all_to_all x1, starting transfers between devices, body(): lax.all_to_all(outgoing.reshape(owners, CAP, width), fsdp, split_axis=0,...  10.5 us
    all_to_all x1, waiting for transfers between devices, body(): lax.all_to_all(outgoing.reshape(owners, CAP, width), fsdp, split_axis=0,...  8.74 us
    all_to_all x1, starting transfers between devices, body(): lax.all_to_all(outgoing_rows.reshape(owners, ys * CAP, width // ys), fsdp...  7.77 us
    all_to_all x1, waiting for transfers between devices, body(): lax.all_to_all(outgoing_rows.reshape(owners, ys * CAP, width // ys), fsdp...  7.76 us
    all_to_all x1, starting transfers between devices, body(): half = lax.all_to_all(half, 'z', split_axis=0, concat_axis=0, tiled=True)  5.9 us
    pallas_call x1, Pallas kernels, ffn(): pl.pallas_call(ffn_kernel, out_shape=(shape, shape), in_specs=[SMEM] + [p...  5.62 us
  transfers between devices with their start and end apart: 38, of which 21 were waited for; matrix products, arithmetic and copies ran while one was open for 5% of the time, Pallas kernels for 8%

profile of v5, /device:TPU:96, one launch (start us, length us, event | category | flops | bytes accessed | tf_op | source)
XLA Modules:
  0.0 182.4 jit_solution(15140344293399344268)
XLA Ops:
  12.3 10.5 %all-to-all-start = ((bf16[32,4,896]{2,1,0:T(4,128)(2,1)}), bf16[32,4,896]{2,1,0:T(4,128)(2,1)S(1)}, u32[]{:S(2)}, u32[]{:S(2)}) async-start(bf16[32,4,896]{2,1,0:T(4,128)(2,1)} %reshape.269), calls=%async_computation | async-start | bytes 458752 | tf_op jit(solution)/shard_map/all_to_all | solution.py:261
  24.0 8.7 %all-to-all-done = bf16[32,4,896]{2,1,0:T(4,128)(2,1)S(1)} async-done(((bf16[32,4,896]{2,1,0:T(4,128)(2,1)}), bf16[32,4,896]{2,1,0:T(4,128)(2,1)S(1)}, u32[]{:S(2)}, u32[]{:S(2)}) %all-to-all-start) | async-done | bytes 229408 | tf_op jit(solution)/shard_map/all_to_all | solution.py:261
  32.9 2.8 %collective-permute-start = (bf16[128,896]{1,0:T(8,128)(2,1)S(1)}, bf16[128,896]{1,0:T(8,128)(2,1)S(1)}, u32[]{:S(2)}, u32[]{:S(2)}) collective-permute-start(bf16[128,896]{1,0:T(8,128)(2,1)S(1)} %reshape.270.refs_0_), channel_id=1, source_target_pairs={{0,192},{64,0},{128,64},{192,128},{1,193},{65,1},{129,65},{193,129... | collective-permute-start | bytes 688136 | tf_op jit(solution)/shard_map/ppermute | solution.py:32
  37.4 5.9 %all-to-all-start.2 = ((bf16[8,64,640]{2,1,0:T(8,128)(2,1)}), bf16[8,64,640]{2,1,0:T(8,128)(2,1)S(1)}, u32[]{:S(2)}, u32[]{:S(2)}) async-start(bf16[8,64,640]{2,1,0:T(8,128)(2,1)} %bitcast.179), calls=%async_computation.2 | async-start | bytes 1310720 | tf_op jit(solution)/shard_map/all_to_all | solution.py:294
  49.2 5.6 %expert_ffn.1 = (bf16[4,128,896]{2,1,0:T(8,128)(2,1)S(1)}, bf16[4,128,896]{2,1,0:T(8,128)(2,1)}) custom-call(s32[8]{0:T(128)S(1)} %pad_add_fusion.order, bf16[128,896]{1,0:T(8,128)(2,1)} %copy-done.4, bf16[128,896]{1,0:T(8,128)(2,1)} %copy-done.6, bf16[128,896]{1,0:T(8,128)(2,1)} %copy-done.7, bf16[128,896]{1,0:T(8,128)(2,1)} %copy-done.8, ...), custom_call_target="tpu_custom_call" | custom-call | tf_op jit(solution)/shard_map/expert_ffn/pallas_call | solution.py:86
  55.1 2.9 %all-to-all-done.2.refs_0_ = bf16[8,64,640]{2,1,0:T(8,128)(2,1)S(1)} async-done(((bf16[8,64,640]{2,1,0:T(8,128)(2,1)}), bf16[8,64,640]{2,1,0:T(8,128)(2,1)S(1)}, u32[]{:S(2)}, u32[]{:S(2)}) %all-to-all-start.2) | async-done | bytes 655392 | tf_op jit(solution)/shard_map/all_to_all | solution.py:294
  65.1 4.3 %collective-permute-done.10.d = bf16[128,896]{1,0:T(8,128)(2,1)S(1)} collective-permute-done((bf16[128,896]{1,0:T(8,128)(2,1)S(1)}, bf16[128,896]{1,0:T(8,128)(2,1)S(1)}, u32[]{:S(2)}, u32[]{:S(2)}) %collective-permute-start.10) | collective-permute-done | bytes 229408 | tf_op jit(solution)/shard_map/ppermute | solution.py:32
  71.4 4.6 %collective-permute-done.9.c = bf16[128,896]{1,0:T(8,128)(2,1)S(1)} collective-permute-done((bf16[128,896]{1,0:T(8,128)(2,1)S(1)}, bf16[128,896]{1,0:T(8,128)(2,1)S(1)}, u32[]{:S(2)}, u32[]{:S(2)}) %collective-permute-start.9) | collective-permute-done | bytes 229408 | tf_op jit(solution)/shard_map/ppermute | solution.py:32
  76.9 3.7 %student.1 = (bf16[1024,640]{1,0:T(8,128)(2,1)}, bf16[8,128,640]{2,1,0:T(8,128)(2,1)}) custom-call(s32[2]{0:T(128)S(1)} %pad_add_fusion.2.order, bf16[8,64,640]{2,1,0:T(8,128)(2,1)S(1)} %all-to-all-done.2.refs_0_, bf16[8,64,640]{2,1,0:T(8,128)(2,1)} %collective-permute-done.11.refs_1_, bf16[4,208,640]{2,1,0:T(8,128)(2,1)S(1)} %bitcast.182), custom_call_target="tpu_custom_call" | custom-call | tf_op jit(solution)/shard_map/student/pallas_call | solution.py:210
  81.4 7.8 %all-to-all-start.1 = ((bf16[32,16,224]{2,1,0:T(8,128)(2,1)}), bf16[32,16,224]{2,1,0:T(8,128)(2,1)S(1)}, u32[]{:S(2)}, u32[]{:S(2)}) async-start(bf16[32,16,224]{2,1,0:T(8,128)(2,1)} %bitcast.22), calls=%async_computation.1 | async-start | bytes 524288 | tf_op jit(solution)/shard_map/all_to_all | solution.py:309
  92.3 7.8 %all-to-all-done.1 = bf16[32,16,224]{2,1,0:T(8,128)(2,1)S(1)} async-done(((bf16[32,16,224]{2,1,0:T(8,128)(2,1)}), bf16[32,16,224]{2,1,0:T(8,128)(2,1)S(1)}, u32[]{:S(2)}, u32[]{:S(2)}) %all-to-all-start.1) | async-done | bytes 229408 | tf_op jit(solution)/shard_map/all_to_all | solution.py:309
  105.4 6.1 %collective-permute-done.12.refs_1_ = bf16[512,224]{1,0:T(8,128)(2,1)S(1)} collective-permute-done((bf16[512,224]{1,0:T(8,128)(2,1)S(1)}, bf16[512,224]{1,0:T(8,128)(2,1)S(1)}, u32[]{:S(2)}, u32[]{:S(2)}) %collective-permute-start.12) | collective-permute-done | bytes 229408 | tf_op jit(solution)/shard_map/ppermute | solution.py:32
  111.5 2.6 %collective-permute-done.13.refs_2_ = bf16[512,224]{1,0:T(8,128)(2,1)S(1)} collective-permute-done((bf16[512,224]{1,0:T(8,128)(2,1)S(1)}, bf16[512,224]{1,0:T(8,128)(2,1)S(1)}, u32[]{:S(2)}, u32[]{:S(2)}) %collective-permute-start.13) | collective-permute-done | bytes 229408 | tf_op jit(solution)/shard_map/ppermute | solution.py:32
  114.1 3.1 %collective-permute-done.14.refs_3_ = bf16[512,224]{1,0:T(8,128)(2,1)S(1)} collective-permute-done((bf16[512,224]{1,0:T(8,128)(2,1)S(1)}, bf16[512,224]{1,0:T(8,128)(2,1)S(1)}, u32[]{:S(2)}, u32[]{:S(2)}) %collective-permute-start.14) | collective-permute-done | bytes 229408 | tf_op jit(solution)/shard_map/ppermute | solution.py:32
  126.0 7.4 %collective-permute-done.19 = bf16[128,640]{1,0:T(8,128)(2,1)S(1)} collective-permute-done((bf16[128,640]{1,0:T(8,128)(2,1)S(1)}, bf16[128,640]{1,0:T(8,128)(2,1)S(1)}, u32[]{:S(2)}, u32[]{:S(2)}) %collective-permute-start.19) | collective-permute-done | bytes 163872 | tf_op jit(solution)/shard_map/ppermute | solution.py:32
  139.3 3.3 %collective-permute-done.22.refs_1_ = bf16[128,640]{1,0:T(8,128)(2,1)S(1)} collective-permute-done((bf16[128,640]{1,0:T(8,128)(2,1)S(1)}, bf16[128,640]{1,0:T(8,128)(2,1)S(1)}, u32[]{:S(2)}, u32[]{:S(2)}) %collective-permute-start.22) | collective-permute-done | bytes 163872 | tf_op jit(solution)/shard_map/ppermute | solution.py:32
  143.0 2.9 %collective-permute-start.27 = (bf16[128,640]{1,0:T(8,128)(2,1)S(1)}, bf16[128,640]{1,0:T(8,128)(2,1)S(1)}, u32[]{:S(2)}, u32[]{:S(2)}) collective-permute-start(bf16[128,640]{1,0:T(8,128)(2,1)S(1)} %collective-permute-done.26.refs_5_), channel_id=1, source_target_pairs={{0,4},{4,8},{8,12},{12,16},{16,20},{20,24},{24,28},{28,0},{1,5},{5... | collective-permute-start | bytes 491528 | tf_op jit(solution)/shard_map/ppermute | solution.py:32
  145.9 3.3 %collective-permute-done.23.refs_2_ = bf16[128,640]{1,0:T(8,128)(2,1)S(1)} collective-permute-done((bf16[128,640]{1,0:T(8,128)(2,1)S(1)}, bf16[128,640]{1,0:T(8,128)(2,1)S(1)}, u32[]{:S(2)}, u32[]{:S(2)}) %collective-permute-start.23) | collective-permute-done | bytes 163872 | tf_op jit(solution)/shard_map/ppermute | solution.py:32
  149.1 3.2 %collective-permute-start.28 = (bf16[128,640]{1,0:T(8,128)(2,1)S(1)}, bf16[128,640]{1,0:T(8,128)(2,1)S(1)}, u32[]{:S(2)}, u32[]{:S(2)}) collective-permute-start(bf16[128,640]{1,0:T(8,128)(2,1)S(1)} %collective-permute-done.27.refs_6_), channel_id=1, source_target_pairs={{0,4},{4,8},{8,12},{12,16},{16,20},{20,24},{24,28},{28,0},{1,5},{5... | collective-permute-start | bytes 491528 | tf_op jit(solution)/shard_map/ppermute | solution.py:32
  152.4 3.7 %collective-permute-done.24.refs_3_ = bf16[128,640]{1,0:T(8,128)(2,1)S(1)} collective-permute-done((bf16[128,640]{1,0:T(8,128)(2,1)S(1)}, bf16[128,640]{1,0:T(8,128)(2,1)S(1)}, u32[]{:S(2)}, u32[]{:S(2)}) %collective-permute-start.24) | collective-permute-done | bytes 163872 | tf_op jit(solution)/shard_map/ppermute | solution.py:32
  156.1 6.5 %collective-permute-done.25.refs_4_ = bf16[128,640]{1,0:T(8,128)(2,1)S(1)} collective-permute-done((bf16[128,640]{1,0:T(8,128)(2,1)S(1)}, bf16[128,640]{1,0:T(8,128)(2,1)S(1)}, u32[]{:S(2)}, u32[]{:S(2)}) %collective-permute-start.25) | collective-permute-done | bytes 163872 | tf_op jit(solution)/shard_map/ppermute | solution.py:32
  165.5 3.6 %collective-permute-start.30 = (bf16[160,640]{1,0:T(8,128)(2,1)S(1)}, bf16[160,640]{1,0:T(8,128)(2,1)S(1)}, u32[]{:S(2)}, u32[]{:S(2)}) collective-permute-start(bf16[160,640]{1,0:T(8,128)(2,1)S(1)} %get-tuple-element.50), channel_id=1, source_target_pairs={{0,2},{1,3},{2,0},{3,1},{4,6},{5,7},{6,4},{7,5},{8,10},{9,11},{10,... | collective-permute-start | bytes 614408 | tf_op jit(solution)/shard_map/ppermute | solution.py:32
  169.1 2.9 %collective-permute-done.29 = bf16[160,640]{1,0:T(8,128)(2,1)S(1)} collective-permute-done((bf16[160,640]{1,0:T(8,128)(2,1)S(1)}, bf16[160,640]{1,0:T(8,128)(2,1)S(1)}, u32[]{:S(2)}, u32[]{:S(2)}) %collective-permute-start.29) | collective-permute-done | bytes 204832 | tf_op jit(solution)/shard_map/ppermute | solution.py:32
  171.9 3.0 %collective-permute-done.30 = bf16[160,640]{1,0:T(8,128)(2,1)S(1)} collective-permute-done((bf16[160,640]{1,0:T(8,128)(2,1)S(1)}, bf16[160,640]{1,0:T(8,128)(2,1)S(1)}, u32[]{:S(2)}, u32[]{:S(2)}) %collective-permute-start.30) | collective-permute-done | bytes 204832 | tf_op jit(solution)/shard_map/ppermute | solution.py:32
  (112 shorter events, 52.2 us)
Async XLA Ops:
  7.2 50.8 %all-gather.6.cloned.1.call-start = ((), (), s32[]{:S(2)}) async-start(), calls=%async_computation.6 | async-start | bytes 1331200 | tf_op jit(solution)/shard_map/all_gather | solution.py:251
  10.5 91.7 %all-gather.4.cloned.1.call-start = ((), (), s32[]{:S(2)}) async-start(), calls=%async_computation.4 | async-start | bytes 2580480 | tf_op jit(solution)/shard_map/all_gather | solution.py:265
  12.3 20.5 %all-to-all-start = ((bf16[32,4,896]{2,1,0:T(4,128)(2,1)}), bf16[32,4,896]{2,1,0:T(4,128)(2,1)S(1)}, u32[]{:S(2)}, u32[]{:S(2)}) async-start(bf16[32,4,896]{2,1,0:T(4,128)(2,1)} %reshape.269), calls=%async_computation | async-start | bytes 458752 | tf_op jit(solution)/shard_map/all_to_all | solution.py:261
  32.9 11.1 %collective-permute-start = (bf16[128,896]{1,0:T(8,128)(2,1)S(1)}, bf16[128,896]{1,0:T(8,128)(2,1)S(1)}, u32[]{:S(2)}, u32[]{:S(2)}) collective-permute-start(bf16[128,896]{1,0:T(8,128)(2,1)S(1)} %reshape.270.refs_0_), channel_id=1, source_target_pairs={{0,192},{64,0},{128,64},{192,128},{1,193},{65,1},{129,65},{193,129... | collective-permute-start | bytes 688136 | tf_op jit(solution)/shard_map/ppermute | solution.py:32
  35.7 9.7 %collective-permute-start.1 = (bf16[128,896]{1,0:T(8,128)(2,1)S(1)}, bf16[128,896]{1,0:T(8,128)(2,1)S(1)}, u32[]{:S(2)}, u32[]{:S(2)}) collective-permute-start(bf16[128,896]{1,0:T(8,128)(2,1)S(1)} %reshape.270.refs_0_), channel_id=1, source_target_pairs={{0,128},{64,192},{128,0},{192,64},{1,129},{65,193},{129,1},{193,65... | collective-permute-start | bytes 688136 | tf_op jit(solution)/shard_map/ppermute | solution.py:32
  36.5 11.2 %collective-permute-start.2 = (bf16[128,896]{1,0:T(8,128)(2,1)S(1)}, bf16[128,896]{1,0:T(8,128)(2,1)S(1)}, u32[]{:S(2)}, u32[]{:S(2)}) collective-permute-start(bf16[128,896]{1,0:T(8,128)(2,1)S(1)} %reshape.270.refs_0_), channel_id=1, source_target_pairs={{0,64},{64,128},{128,192},{192,0},{1,65},{65,129},{129,193},{193,1... | collective-permute-start | bytes 688136 | tf_op jit(solution)/shard_map/ppermute | solution.py:32
  37.4 20.6 %all-to-all-start.2 = ((bf16[8,64,640]{2,1,0:T(8,128)(2,1)}), bf16[8,64,640]{2,1,0:T(8,128)(2,1)S(1)}, u32[]{:S(2)}, u32[]{:S(2)}) async-start(bf16[8,64,640]{2,1,0:T(8,128)(2,1)} %bitcast.179), calls=%async_computation.2 | async-start | bytes 1310720 | tf_op jit(solution)/shard_map/all_to_all | solution.py:294
  43.3 90.8 %reduce-scatter.2.cloned.1.call-start = ((), (), s32[]{:S(2)}) async-start(), calls=%async_computation.5 | async-start | bytes 1474560 | tf_op jit(solution)/shard_map/reduce_scatter | solution.py:308
  58.0 18.9 %collective-permute-start.11 = (bf16[8,64,640]{2,1,0:T(8,128)(2,1)S(1)}, bf16[8,64,640]{2,1,0:T(8,128)(2,1)}, u32[]{:S(2)}, u32[]{:S(2)}) collective-permute-start(bf16[8,64,640]{2,1,0:T(8,128)(2,1)S(1)} %all-to-all-done.2.refs_0_), channel_id=1, source_target_pairs={{0,32},{32,0},{1,33},{33,1},{2,34},{34,2},{3,35},{35,3},{4,36},{36... | collective-permute-start | bytes 1966088 | tf_op jit(solution)/shard_map/ppermute | solution.py:32
  60.3 9.1 %collective-permute-start.10 = (bf16[128,896]{1,0:T(8,128)(2,1)S(1)}, bf16[128,896]{1,0:T(8,128)(2,1)S(1)}, u32[]{:S(2)}, u32[]{:S(2)}) collective-permute-start(bf16[128,896]{1,0:T(8,128)(2,1)S(1)} %get-tuple-element.52), channel_id=1, source_target_pairs={{0,192},{64,0},{128,64},{192,128},{1,193},{65,1},{129,65},{193,129... | collective-permute-start | bytes 688136 | tf_op jit(solution)/shard_map/ppermute | solution.py:32
  62.1 9.3 %collective-permute-start.8 = (bf16[128,896]{1,0:T(8,128)(2,1)S(1)}, bf16[128,896]{1,0:T(8,128)(2,1)S(1)}, u32[]{:S(2)}, u32[]{:S(2)}) collective-permute-start(bf16[128,896]{1,0:T(8,128)(2,1)S(1)} %get-tuple-element.54), channel_id=1, source_target_pairs={{0,64},{64,128},{128,192},{192,0},{1,65},{65,129},{129,193},{193,1... | collective-permute-start | bytes 688136 | tf_op jit(solution)/shard_map/ppermute | solution.py:32
  63.1 12.9 %collective-permute-start.9 = (bf16[128,896]{1,0:T(8,128)(2,1)S(1)}, bf16[128,896]{1,0:T(8,128)(2,1)S(1)}, u32[]{:S(2)}, u32[]{:S(2)}) collective-permute-start(bf16[128,896]{1,0:T(8,128)(2,1)S(1)} %get-tuple-element.53), channel_id=1, source_target_pairs={{0,128},{64,192},{128,0},{192,64},{1,129},{65,193},{129,1},{193,65... | collective-permute-start | bytes 688136 | tf_op jit(solution)/shard_map/ppermute | solution.py:32
  81.4 18.7 %all-to-all-start.1 = ((bf16[32,16,224]{2,1,0:T(8,128)(2,1)}), bf16[32,16,224]{2,1,0:T(8,128)(2,1)S(1)}, u32[]{:S(2)}, u32[]{:S(2)}) async-start(bf16[32,16,224]{2,1,0:T(8,128)(2,1)} %bitcast.22), calls=%async_computation.1 | async-start | bytes 524288 | tf_op jit(solution)/shard_map/all_to_all | solution.py:309
  102.2 9.3 %collective-permute-start.12 = (bf16[512,224]{1,0:T(8,128)(2,1)S(1)}, bf16[512,224]{1,0:T(8,128)(2,1)S(1)}, u32[]{:S(2)}, u32[]{:S(2)}) collective-permute-start(bf16[512,224]{1,0:T(8,128)(2,1)S(1)} %convolution_convert_fusion.refs_0_), channel_id=1, source_target_pairs={{0,192},{64,0},{128,64},{192,128},{1,193},{65,1},{129,65},{193,129... | collective-permute-start | bytes 688136 | tf_op jit(solution)/shard_map/ppermute | solution.py:32
  103.4 10.7 %collective-permute-start.13 = (bf16[512,224]{1,0:T(8,128)(2,1)S(1)}, bf16[512,224]{1,0:T(8,128)(2,1)S(1)}, u32[]{:S(2)}, u32[]{:S(2)}) collective-permute-start(bf16[512,224]{1,0:T(8,128)(2,1)S(1)} %convolution_convert_fusion.refs_0_), channel_id=1, source_target_pairs={{0,128},{64,192},{128,0},{192,64},{1,129},{65,193},{129,1},{193,65... | collective-permute-start | bytes 688136 | tf_op jit(solution)/shard_map/ppermute | solution.py:32
  104.4 12.8 %collective-permute-start.14 = (bf16[512,224]{1,0:T(8,128)(2,1)S(1)}, bf16[512,224]{1,0:T(8,128)(2,1)S(1)}, u32[]{:S(2)}, u32[]{:S(2)}) collective-permute-start(bf16[512,224]{1,0:T(8,128)(2,1)S(1)} %convolution_convert_fusion.refs_0_), channel_id=1, source_target_pairs={{0,64},{64,128},{128,192},{192,0},{1,65},{65,129},{129,193},{193,1... | collective-permute-start | bytes 688136 | tf_op jit(solution)/shard_map/ppermute | solution.py:32
  105.4 13.6 %collective-permute-start.15 = (bf16[512,224]{1,0:T(8,128)(2,1)S(1)}, bf16[512,224]{1,0:T(8,128)(2,1)S(1)}, u32[]{:S(2)}, u32[]{:S(2)}) collective-permute-start(bf16[512,224]{1,0:T(8,128)(2,1)S(1)} %convolution_convert_fusion.refs_0_), channel_id=1, source_target_pairs={{0,32},{32,0},{1,33},{33,1},{2,34},{34,2},{3,35},{35,3},{4,36},{36... | collective-permute-start | bytes 688136 | tf_op jit(solution)/shard_map/ppermute | solution.py:32
  111.5 7.5 %collective-permute-start.16 = (bf16[512,224]{1,0:T(8,128)(2,1)S(1)}, bf16[512,224]{1,0:T(8,128)(2,1)S(1)}, u32[]{:S(2)}, u32[]{:S(2)}) collective-permute-start(bf16[512,224]{1,0:T(8,128)(2,1)S(1)} %collective-permute-done.12.refs_1_), channel_id=1, source_target_pairs={{0,32},{32,0},{1,33},{33,1},{2,34},{34,2},{3,35},{35,3},{4,36},{36... | collective-permute-start | bytes 688136 | tf_op jit(solution)/shard_map/ppermute | solution.py:32
  122.2 11.2 %collective-permute-start.19 = (bf16[128,640]{1,0:T(8,128)(2,1)S(1)}, bf16[128,640]{1,0:T(8,128)(2,1)S(1)}, u32[]{:S(2)}, u32[]{:S(2)}) collective-permute-start(bf16[128,640]{1,0:T(8,128)(2,1)S(1)} %get-tuple-element.43), channel_id=1, source_target_pairs={{0,1},{1,2},{2,3},{3,0},{4,5},{5,6},{6,7},{7,4},{8,9},{9,10},{10,1... | collective-permute-start | bytes 491528 | tf_op jit(solution)/shard_map/ppermute | solution.py:32
  122.2 11.2 %collective-permute-start.20 = (bf16[128,640]{1,0:T(8,128)(2,1)S(1)}, bf16[128,640]{1,0:T(8,128)(2,1)S(1)}, u32[]{:S(2)}, u32[]{:S(2)}) collective-permute-start(bf16[128,640]{1,0:T(8,128)(2,1)S(1)} %get-tuple-element.44), channel_id=1, source_target_pairs={{0,2},{1,3},{2,0},{3,1},{4,6},{5,7},{6,4},{7,5},{8,10},{9,11},{10,... | collective-permute-start | bytes 491528 | tf_op jit(solution)/shard_map/ppermute | solution.py:32
  124.7 9.4 %collective-permute-start.21 = (bf16[128,640]{1,0:T(8,128)(2,1)S(1)}, bf16[128,640]{1,0:T(8,128)(2,1)}, u32[]{:S(2)}, u32[]{:S(2)}) collective-permute-start(bf16[128,640]{1,0:T(8,128)(2,1)S(1)} %get-tuple-element.45), channel_id=1, source_target_pairs={{0,3},{1,0},{2,1},{3,2},{4,7},{5,4},{6,5},{7,6},{8,11},{9,8},{10,9... | collective-permute-start | bytes 491528 | tf_op jit(solution)/shard_map/ppermute | solution.py:32
  149.1 6.9 %collective-permute-start.24 = (bf16[128,640]{1,0:T(8,128)(2,1)S(1)}, bf16[128,640]{1,0:T(8,128)(2,1)S(1)}, u32[]{:S(2)}, u32[]{:S(2)}) collective-permute-start(bf16[128,640]{1,0:T(8,128)(2,1)S(1)} %collective-permute-done.23.refs_2_), channel_id=1, source_target_pairs={{0,28},{4,0},{8,4},{12,8},{16,12},{20,16},{24,20},{28,24},{1,29},{... | collective-permute-start | bytes 491528 | tf_op jit(solution)/shard_map/ppermute | solution.py:32
  164.5 7.4 %collective-permute-start.29 = (bf16[160,640]{1,0:T(8,128)(2,1)S(1)}, bf16[160,640]{1,0:T(8,128)(2,1)S(1)}, u32[]{:S(2)}, u32[]{:S(2)}) collective-permute-start(bf16[160,640]{1,0:T(8,128)(2,1)S(1)} %get-tuple-element.49), channel_id=1, source_target_pairs={{0,1},{1,2},{2,3},{3,0},{4,5},{5,6},{6,7},{7,4},{8,9},{9,10},{10,1... | collective-permute-start | bytes 614408 | tf_op jit(solution)/shard_map/ppermute | solution.py:32
  165.5 9.5 %collective-permute-start.30 = (bf16[160,640]{1,0:T(8,128)(2,1)S(1)}, bf16[160,640]{1,0:T(8,128)(2,1)S(1)}, u32[]{:S(2)}, u32[]{:S(2)}) collective-permute-start(bf16[160,640]{1,0:T(8,128)(2,1)S(1)} %get-tuple-element.50), channel_id=1, source_target_pairs={{0,2},{1,3},{2,0},{3,1},{4,6},{5,7},{6,4},{7,5},{8,10},{9,11},{10,... | collective-permute-start | bytes 614408 | tf_op jit(solution)/shard_map/ppermute | solution.py:32
  (23 other events, 133.1 us)
Sparse Core Ops, SparseCore 0:
  10.7 29.3 all-gather.5
  41.9 42.0 all-gather.3
  86.5 37.6 reduce-scatter.1
